TPU v7x, 1024 devices: a whole 8x8x8 slice. The times are simulated.
1024 devices in a mesh: grp: 2 (over z_lo), ta: 8 (over y), xyz: 64 (over z_hi, x, core).
Axes of the slice: x: 8, y: 8, z: 8 (z_hi: 4, z_lo: 2; z = z_hi * 2 + z_lo), core: 2. Of those that a mesh axis runs over, the one named last changes fastest.
Arguments:
- links: float32 [4, 3, 3, 2, 16, 64, 256], P(None, None, None, None, ('grp', 'ta'), 'xyz'), may hold values from -1 to 1, as said below
- momenta: float32 [4, 3, 3, 2, 16, 64, 256], P(None, None, None, None, ('grp', 'ta'), 'xyz'), may hold values from -11 to 11, as said below
- vectors: float32 [16, 3, 2, 2, 8, 64, 256], P('grp', None, None, None, 'ta', 'xyz'), may hold values from -6 to 6
- coefficients: float32 [4], replicated, may hold values from -1 to 1
Outputs:
- new_links: float32 [4, 3, 3, 2, 16, 64, 256], P(None, None, None, None, ('grp', 'ta'), 'xyz')
- new_momenta: float32 [4, 3, 3, 2, 16, 64, 256], P(None, None, None, None, ('grp', 'ta'), 'xyz')
- filtered: float32 [16, 3, 2, 2, 8, 64, 256], P('grp', None, None, None, 'ta', 'xyz')
Inputs may be any that keep to these rules, and one draw needn't show every extreme that they name: `links`: every 3 x 3 link matrix is special unitary up to rounding. `momenta`: every 3 x 3 momentum matrix is anti-Hermitian and traceless: an entry below the diagonal has exactly the negated real part and the same imaginary part as its mirror above, the diagonal has zero real parts.
All inputs are finite; a program needn't handle non-finite values.
Results may differ from a plain program's by a relative error of at most 0.0001.
Values sent between devices are 32-bit elements; how exact they have to be, the bound alone decides.
No kernel may reach another device: no remote copies, remote signals or barrier semaphores. Data moves between devices by JAX's collectives and lax.ppermute only.
A program may use at most 64 MiB of HBM per device.

v0:
```python
import functools

import jax
import jax.numpy as jnp
from jax import lax
from jax.experimental import pallas as pl
from jax.experimental.pallas import tpu as pltpu
from jax.sharding import PartitionSpec as P

NZ = 32
NSTEP = 2
NCHEB = 3
coupling = 5.7
time_step = 0.1
taylor_degree = 6

AXES = ("grp", "ta", "xyz")
TILE = (8, 128)
F32 = jnp.float32


def roll(value, shift, axis):
    return pltpu.roll(value, shift % value.shape[axis], axis)


def iotas():
    row = lax.broadcasted_iota(jnp.int32, TILE, 0)
    lane = lax.broadcasted_iota(jnp.int32, TILE, 1)
    return row, lane


def load_matrix(entry):
    return [[(entry((i * 3 + j) * 2), entry((i * 3 + j) * 2 + 1)) for j in range(3)] for i in range(3)]


def product(left, right, left_h=False, right_h=False):
    out = []
    for i in range(3):
        line = []
        for j in range(3):
            real, imag = None, None
            for k in range(3):
                ar, ai = left[k][i] if left_h else left[i][k]
                br, bi = right[j][k] if right_h else right[k][j]
                rr, ii, ri, ir = ar * br, ai * bi, ar * bi, ai * br
                re = rr + ii if left_h != right_h else rr - ii
                if left_h and right_h:
                    im_terms = (-1, ri, ir)
                elif left_h:
                    im_terms = (1, ri, -1, ir)
                elif right_h:
                    im_terms = (1, ir, -1, ri)
                else:
                    im_terms = (1, ri, ir)
                real = re if real is None else real + re
                if len(im_terms) == 4:
                    im = im_terms[1] - im_terms[3]
                    imag = im if imag is None else imag + im
                else:
                    im = im_terms[1] + im_terms[2]
                    if im_terms[0] < 0:
                        imag = -im if imag is None else imag - im
                    else:
                        imag = im if imag is None else imag + im
            line.append((real, imag))
        out.append(line)
    return out


def exponential(packed, scale):
    a0, a1, r01, s01, r02, s02, r12, s12 = [packed(c) * scale for c in range(8)]
    a2 = -(a0 + a1)
    h01, h02, h12 = (s01, -r01), (s02, -r02), (s12, -r12)
    n01, n02, n12 = (s01 * s01 + r01 * r01, s02 * s02 + r02 * r02, s12 * s12 + r12 * r12)
    d0, d1, d2 = a0 * a0, a1 * a1, a2 * a2
    p = 0.5 * (d0 + d1 + d2) + (n01 + n02 + n12)

    def cmul(x, y):
        return (x[0] * y[0] - x[1] * y[1], x[0] * y[1] + x[1] * y[0])

    def cmul_conj(x, y):
        return (x[0] * y[0] + x[1] * y[1], x[1] * y[0] - x[0] * y[1])

    m = cmul(h01, h12)
    q = a0 * a1 * a2 + 2.0 * (m[0] * h02[0] + m[1] * h02[1]) - a0 * n12 - a1 * n02 - a2 * n01
    k01 = cmul_conj(h02, h12)
    k12 = cmul_conj(h02, h01)
    g01 = (k01[0] - a2 * h01[0], k01[1] - a2 * h01[1])
    g02 = (m[0] - a1 * h02[0], m[1] - a1 * h02[1])
    g12 = (k12[0] - a0 * h12[0], k12[1] - a0 * h12[1])
    g00, g11, g22 = d0 + n01 + n02, d1 + n01 + n12, d2 + n02 + n12
    assert taylor_degree == 6
    c2 = -1.0 / 30.0
    f0 = (None, (c2 / 4.0) * q)
    f1 = (None, 0.25 + (c2 / 4.0) * p)
    f2r = -1.0 / 20.0
    t0 = f2r * q
    u0r, u0i = 1.0 + f2r * p, f0[1]
    w = f1[1]
    f0 = (1.0, t0 * (1.0 / 3.0))
    f1 = (-u0i * (1.0 / 3.0), u0r * (1.0 / 3.0))
    f2 = (-w * (1.0 / 3.0), None)
    t0 = f2[0] * q
    u0r, u0i = 1.0 + f2[0] * p, f0[1]
    f0 = (1.0, t0 * 0.5)
    f2 = (-f1[1] * 0.5, f1[0] * 0.5)
    f1 = (-u0i * 0.5, u0r * 0.5)
    f0, f1, f2 = (
        (1.0 - f2[1] * q, f2[0] * q),
        (-(f0[1] + f2[1] * p), 1.0 + f2[0] * p),
        (-f1[1], f1[0]),
    )

    def pair(h, g):
        rr = f1[0] * h[0] + f2[0] * g[0]
        ii = f1[1] * h[1] + f2[1] * g[1]
        ri = f1[0] * h[1] + f2[0] * g[1]
        ir = f1[1] * h[0] + f2[1] * g[0]
        return (rr - ii, ri + ir), (rr + ii, ir - ri)

    def diag(a, g):
        return (f0[0] + f1[0] * a + f2[0] * g, f0[1] + f1[1] * a + f2[1] * g)

    e01, e10 = pair(h01, g01)
    e02, e20 = pair(h02, g02)
    e12, e21 = pair(h12, g12)
    return [
        [diag(a0, g00), e01, e02],
        [e10, diag(a1, g11), e12],
        [e20, e21, diag(a2, g22)],
    ]


def store_matrix(ref, lead, matrix):
    for i in range(3):
        for j in range(3):
            for part in range(2):
                ref[lead + ((i * 3 + j) * 2 + part,)] = matrix[i][j][part]


def updated(packed, entry):
    return product(exponential(packed, time_step), load_matrix(entry))


def link_shift_y(value, amount, row, lane):
    if amount == 1:
        rolled = roll(value, -NZ, 1)
        inside = lane < 128 - NZ
    else:
        rolled = roll(value, NZ, 1)
        inside = lane >= NZ
    other = jnp.where(row % 2 == 1, roll(rolled, 1, 0), roll(rolled, -1, 0))
    return jnp.where(inside, rolled, other)


def vector_shift_y(value, amount, lane):
    if amount == 1:
        rolled = roll(value, -NZ, 1)
        inside = lane < 128 - NZ
    else:
        rolled = roll(value, NZ, 1)
        inside = lane >= NZ
    return jnp.where(inside, rolled, roll(rolled, 4, 0))


def shift_z(value, amount, lane):
    if amount == 1:
        return jnp.where(lane % NZ == NZ - 1, roll(value, NZ - 1, 1), roll(value, -1, 1))
    return jnp.where(lane % NZ == 0, roll(value, -(NZ - 1), 1), roll(value, 1, 1))


def force(own, halo, forward, work):
    row, lane = iotas()
    direction = row // 2
    is_dir = [direction == d for d in range(4)]
    for c in range(18):
        value = own(c)
        ahead = [
            halo(0, c),
            halo(2, c),
            link_shift_y(value, 1, row, lane),
            shift_z(value, 1, lane),
        ]
        for k in range(1, 4):
            forward[k - 1, c] = jnp.where(
                is_dir[0],
                ahead[k % 4],
                jnp.where(
                    is_dir[1], ahead[(1 + k) % 4], jnp.where(is_dir[2], ahead[(2 + k) % 4], ahead[(3 + k) % 4])
                ),
            )

    def turned(value, k):
        return roll(value, -2 * k, 0)

    def base(c):
        return jnp.where(is_dir[0], halo(1, c), jnp.where(is_dir[1], halo(3, c), own(c)))

    def corner_ahead(k, c):
        plain = turned(forward[3 - k, c], k)
        if k == 1:
            moved = turned(shift_z(turned(base(c), 2), 1, lane), -1)
            return jnp.where(is_dir[3], moved, jnp.where(is_dir[0], halo(0, c), plain))
        start = turned(base(c), 2)
        if k == 2:
            return jnp.where(
                is_dir[2],
                link_shift_y(start, 1, row, lane),
                jnp.where(is_dir[3], shift_z(start, 1, lane), plain),
            )
        moved = turned(link_shift_y(start, 1, row, lane), 1)
        return jnp.where(is_dir[1], halo(2, c), jnp.where(is_dir[2], moved, plain))

    def here(k, c):
        value = own(c)
        time_row, space_row = {1: (3, 0), 2: (2, 3), 3: (1, 2)}[k]
        return jnp.where(is_dir[time_row], halo(1, c), jnp.where(is_dir[space_row], halo(3, c), value))

    for k in range(1, 4):
        up = product(
            load_matrix(lambda c: turned(forward[3 - k, c], k)),
            load_matrix(lambda c: forward[k - 1, c]),
            right_h=True,
        )
        up = product(up, load_matrix(lambda c: turned(own(c), k)), right_h=True)
        low = product(load_matrix(lambda c: here(k, c)), load_matrix(lambda c: corner_ahead(k, c)))
        low = product(low, load_matrix(lambda c: turned(base(c), k)), left_h=True)
        direct = {1: is_dir[0] | is_dir[3], 2: is_dir[2] | is_dir[3], 3: is_dir[1] | is_dir[2]}[k]
        for c in range(18):
            i, j, part = c // 6, (c // 2) % 3, c % 2
            staple, down = up[i][j][part], low[i][j][part]
            staple = staple + jnp.where(direct, down, 0.0)
            if k == 1:
                work[0, c], work[1, c], work[2, c] = staple, down, down
            else:
                y_row, z_row = {2: (0, 1), 3: (3, 0)}[k]
                work[0, c] = work[0, c] + staple
                work[1, c] = jnp.where(is_dir[y_row], down, work[1, c])
                work[2, c] = jnp.where(is_dir[z_row], down, work[2, c])

    def staples(c):
        y_part = jnp.where(is_dir[2], 0.0, link_shift_y(work[1, c], -1, row, lane))
        z_part = jnp.where(is_dir[3], 0.0, shift_z(work[2, c], -1, lane))
        return work[0, c] + y_part + z_part

    total = product(load_matrix(own), load_matrix(staples))
    mean = (total[0][0][1] + total[1][1][1] + total[2][2][1]) * (1.0 / 3.0)
    factor = coupling / 3.0
    out = [(total[0][0][1] - mean) * factor, (total[1][1][1] - mean) * factor]
    for i, j in ((0, 1), (0, 2), (1, 2)):
        out.append((total[i][j][0] - total[j][i][0]) * (0.5 * factor))
        out.append((total[i][j][1] + total[j][i][1]) * (0.5 * factor))
    return out


def halo_entries(place, count, pair_ref, sides_ref, across_ref):
    row, _ = iotas()
    odd_time, odd_space = place
    first = odd_space == 0

    def corner(c):
        value = across_ref[odd_space, count + c // 2]
        return roll(value, 4, 0) if c % 2 else value

    def entry(h, c):
        if h == 0:
            value = sides_ref[odd_time, 1, odd_space, c]
            extra = jnp.where(first, corner(c), sides_ref[odd_time, 1, 1 - odd_space, c])
            return jnp.where(row < 2, roll(extra, -2, 0), value)
        if h == 1:
            return sides_ref[1 - odd_time, 0, odd_space, c]
        near, far = pair_ref[1 - odd_space, c], across_ref[odd_space, c]
        if h == 2:
            value = jnp.where(first, near, far)
            extra = jnp.where(first, sides_ref[1 - odd_time, 0, 1 - odd_space, c], corner(c))
            return jnp.where(row // 2 == 1, roll(extra, 2, 0), value)
        return jnp.where(first, far, near)

    return entry


def split_kernel(place_ref, links_ref, momenta_ref, vectors_ref, own_ref, packed_ref, fields_ref):
    half = place_ref[2]
    for c in range(18):
        for d in range(4):
            own_ref[c, 2 * d : 2 * d + 2, :] = links_ref[d * 36 + 2 * c : d * 36 + 2 * c + 2, :]
    for slot, c in enumerate(PACKED):
        for d in range(4):
            packed_ref[slot, 2 * d : 2 * d + 2, :] = momenta_ref[d * 36 + 2 * c : d * 36 + 2 * c + 2, :]
    for c in range(6):
        for block in range(2):
            tiles = []
            for h in range(2):
                parts = [
                    vectors_ref[pl.ds(block * 96 + c * 4 + h * 2 + side, 4, stride=24), :] for side in range(2)
                ]
                tiles.append(jnp.concatenate(parts, axis=0))
            fields_ref[c * 4 + block] = jnp.where(half == 0, tiles[0], tiles[1])
            fields_ref[c * 4 + 2 + block] = jnp.where(half == 0, tiles[1], tiles[0])


PACKED = (1, 9, 2, 3, 4, 5, 10, 11)


def bundle_kernel(count, extra, place_ref, own_ref, sides_ref, *rest):
    row, _ = iotas()
    odd_time, odd_space = place_ref[0], place_ref[1]
    out_ref = rest[-1]

    def corner(c):
        ahead = sides_ref[odd_time, 1, odd_space, c]
        behind = sides_ref[1 - odd_time, 0, odd_space, c]
        return jnp.where(row < 2, behind, ahead)

    for c in range(count):
        out_ref[c] = own_ref[c]
    for pair in range(count // 2):
        out_ref[count + pair] = jnp.where(row < 4, corner(2 * pair), roll(corner(2 * pair + 1), 4, 0))
    for c in range(extra):
        out_ref[count + count // 2 + c] = rest[0][c]


def first_kernel(place_ref, own_ref, packed_ref, pair_ref, sides_ref, across_ref, halo_ref, next_ref, forward, work):
    entry = halo_entries((place_ref[0], place_ref[1]), 18, pair_ref, sides_ref, across_ref)
    for h in range(4):
        for c in range(18):
            halo_ref[h, c] = entry(h, c)
    kick = force(lambda c: own_ref[c], lambda h, c: halo_ref[h, c], forward, work)
    for c in range(8):
        next_ref[c] = packed_ref[c] - (0.5 * time_step) * kick[c]


def drift(place_ref, own_ref, halo_ref, packed_ref, pair_ref, sides_ref, across_ref, new_own_ref, new_halo_ref):
    entry = halo_entries((place_ref[0], place_ref[1]), 8, pair_ref, sides_ref, across_ref)
    store_matrix(new_own_ref, (), updated(lambda c: packed_ref[c], lambda c: own_ref[c]))
    for h in range(4):
        store_matrix(new_halo_ref, (h,), updated(lambda c: entry(h, c), lambda c: halo_ref[h, c]))


def middle_kernel(
    place_ref, own_ref, halo_ref, packed_ref, pair_ref, sides_ref, across_ref,
    new_own_ref, new_halo_ref, next_ref, forward, work,
):
    drift(place_ref, own_ref, halo_ref, packed_ref, pair_ref, sides_ref, across_ref, new_own_ref, new_halo_ref)
    kick = force(lambda c: new_own_ref[c], lambda h, c: new_halo_ref[h, c], forward, work)
    for c in range(8):
        next_ref[c] = packed_ref[c] - time_step * kick[c]


def last_drift_kernel(
    place_ref, own_ref, halo_ref, packed_ref, pair_ref, sides_ref, across_ref, new_own_ref, new_halo_ref, spatial_ref
):
    drift(place_ref, own_ref, halo_ref, packed_ref, pair_ref, sides_ref, across_ref, new_own_ref, new_halo_ref)
    row, _ = iotas()
    for c in range(18):
        spatial_ref[c] = jnp.where(row < 2, roll(new_halo_ref[3, c], -2, 0), new_own_ref[c])


def last_force_kernel(own_ref, halo_ref, packed_ref, links_ref, momenta_ref, forward, work):
    kick = force(lambda c: own_ref[c], lambda h, c: halo_ref[h, c], forward, work)
    final = [packed_ref[c] - (0.5 * time_step) * kick[c] for c in range(8)]
    a0, a1, r01, s01, r02, s02, r12, s12 = final
    zero = jnp.zeros(TILE, F32)
    full = [zero, a0, r01, s01, r02, s02, -r01, s01, zero, a1, r12, s12, -r02, s02, -r12, s12, zero, -(a0 + a1)]
    for c in range(18):
        value = own_ref[c]
        for d in range(4):
            links_ref[d * 36 + 2 * c : d * 36 + 2 * c + 2, :] = value[2 * d : 2 * d + 2, :]
            momenta_ref[d * 36 + 2 * c : d * 36 + 2 * c + 2, :] = full[c][2 * d : 2 * d + 2, :]


def hopping(place_ref, spatial_ref, field_ref, near_ref, across_ref, offset, emit):
    row, lane = iotas()
    odd_space, half = place_ref[1], place_ref[2]
    first = odd_space == 0
    for side in range(2):
        owner = half if side == 0 else 1 - half

        def link(d, c):
            low = jnp.broadcast_to(spatial_ref[owner, c, 2 * d : 2 * d + 1, :], TILE)
            high = jnp.broadcast_to(spatial_ref[owner, c, 2 * d + 1 : 2 * d + 2, :], TILE)
            return jnp.where(row < 4, low, high)

        totals = {}
        for d in range(4):
            matrix = load_matrix(lambda c: link(d, c))
            for block in range(2):
                def tile(c):
                    return c * 4 + side * 2 + block

                def times(vector, dagger):
                    out = []
                    for i in range(3):
                        real, imag = None, None
                        for k in range(3):
                            ar, ai = matrix[k][i] if dagger else matrix[i][k]
                            br, bi = vector[2 * k], vector[2 * k + 1]
                            if dagger:
                                re, im = ar * br + ai * bi, ar * bi - ai * br
                            else:
                                re, im = ar * br - ai * bi, ar * bi + ai * br
                            real = re if real is None else real + re
                            imag = im if imag is None else imag + im
                        out += [real, imag]
                    return out

                if d < 2:
                    vector = []
                    for c in range(6):
                        near, far = near_ref[1 - odd_space, tile(c)], across_ref[odd_space, offset + tile(c)]
                        vector.append(jnp.where(first, near, far) if d == 1 else jnp.where(first, far, near))
                    parts = [times(vector, d == 0)]
                else:
                    values = [field_ref[tile(c)] for c in range(6)]
                    back = times(values, True)
                    if d == 2:
                        ahead = times([vector_shift_y(v, 1, lane) for v in values], False)
                        parts = [ahead, [vector_shift_y(v, -1, lane) for v in back]]
                    else:
                        ahead = times([shift_z(v, 1, lane) for v in values], False)
                        parts = [ahead, [shift_z(v, -1, lane) for v in back]]
                for part in parts:
                    for c in range(6):
                        old = totals.get((block, c))
                        totals[block, c] = part[c] if old is None else old + part[c]
        for block in range(2):
            for c in range(6):
                emit(c * 4 + side * 2 + block, totals[block, c] * (-1.0 / 6.0))


def first_hop_kernel(offset, place_ref, spatial_ref, field_ref, near_ref, across_ref, out_ref):
    def emit(tile, value):
        out_ref[tile] = value

    hopping(place_ref, spatial_ref, field_ref, near_ref, across_ref, offset, emit)


def next_hop_kernel(place_ref, spatial_ref, field_ref, older_ref, near_ref, across_ref, out_ref):
    def emit(tile, value):
        out_ref[tile] = 2.0 * value - older_ref[tile]

    hopping(place_ref, spatial_ref, field_ref, near_ref, across_ref, 0, emit)


def last_hop_kernel(
    place_ref, coefficients_ref, spatial_ref, field_ref, older_ref, oldest_ref, near_ref, across_ref, out_ref, work
):
    half = place_ref[2]

    def emit(tile, value):
        newest = 2.0 * value - older_ref[tile]
        total = coefficients_ref[0] * oldest_ref[tile] + coefficients_ref[1] * older_ref[tile]
        work[tile] = total + coefficients_ref[2] * field_ref[tile] + coefficients_ref[3] * newest

    hopping(place_ref, spatial_ref, field_ref, near_ref, across_ref, 0, emit)
    for c in range(6):
        for block in range(2):
            mine, theirs = work[c * 4 + block], work[c * 4 + 2 + block]
            for h in range(2):
                value = jnp.where(half == h, mine, theirs)
                for side in range(2):
                    out_ref[pl.ds(block * 96 + c * 4 + h * 2 + side, 4, stride=24), :] = value[4 * side : 4 * side + 4, :]


def call(kernel, shapes, inputs, scratch=(), scalars=1):
    smem = pl.BlockSpec(memory_space=pltpu.SMEM)
    vmem = pl.BlockSpec(memory_space=pltpu.VMEM)
    outs = [jax.ShapeDtypeStruct(shape, F32) for shape in shapes]
    result = pl.pallas_call(
        kernel,
        out_shape=outs,
        in_specs=[smem] * scalars + [vmem] * (len(inputs) - scalars),
        out_specs=[vmem] * len(outs),
        scratch_shapes=[pltpu.VMEM(shape + TILE, F32) for shape in scratch],
    )(*inputs)
    return result


def pairs(mesh):
    times, spaces = mesh.shape["grp"] * mesh.shape["ta"], mesh.shape["xyz"]
    offset = mesh.shape["ta"]

    def at(t, x):
        return (t % times) * spaces + x % spaces

    chip = [[at(t, x), at(t, x + 1)] for t in range(times) for x in range(0, spaces, 2)]
    across = [[at(t, x), at(t, x + 1)] for t in range(times) for x in range(1, spaces, 2)]
    time = [[at(t, x), at(t + 1, x)] for x in range(spaces) for t in range(x % 2, times, 2)]
    halves = [[at(t, x), at(t + offset, x)] for t in range(offset) for x in range(spaces)]
    return chip, across, time, halves


def body(groups, links, momenta, vectors, coefficients):
    chip, across, time, halves = groups

    def meet(values, which):
        return lax.all_gather(values, AXES, axis_index_groups=which)

    t = lax.axis_index(("grp", "ta"))
    x = lax.axis_index("xyz")
    place = jnp.stack([t % 2, x % 2, lax.axis_index("grp")]).astype(jnp.int32)
    own, packed, fields = call(
        split_kernel,
        [(18,) + TILE, (8,) + TILE, (24,) + TILE],
        [place, links.reshape(144, 128), momenta.reshape(144, 128), vectors.reshape(192, 128)],
    )
    forces = [(3, 18), (3, 18)]

    def exchange(values, extra=None):
        count = values.shape[0]
        near = meet(values, chip)
        sides = meet(meet(near, time), chip)
        inputs = [place, values, sides] + ([] if extra is None else [extra])
        more = 0 if extra is None else extra.shape[0]
        (sent,) = call(
            functools.partial(bundle_kernel, count, more), [(count + count // 2 + more,) + TILE], inputs
        )
        return near, sides, meet(sent, across)

    near, sides, far = exchange(own, fields)
    fields_near, fields_far = meet(fields, chip), far
    halo, packed = call(
        first_kernel, [(4, 18) + TILE, (8,) + TILE], [place, own, packed, near, sides, far], forces
    )
    own, halo, packed = call(
        middle_kernel,
        [(18,) + TILE, (4, 18) + TILE, (8,) + TILE],
        [place, own, halo, packed, *exchange(packed)],
        forces,
    )
    own, halo, spatial = call(
        last_drift_kernel,
        [(18,) + TILE, (4, 18) + TILE, (18,) + TILE],
        [place, own, halo, packed, *exchange(packed)],
    )
    spatial = meet(spatial, halves)
    (one,) = call(
        functools.partial(first_hop_kernel, 27),
        [(24,) + TILE],
        [place, spatial, fields, fields_near, fields_far],
    )
    (two,) = call(
        next_hop_kernel,
        [(24,) + TILE],
        [place, spatial, one, fields, meet(one, chip), meet(one, across)],
    )
    new_links, new_momenta = call(
        last_force_kernel, [(144, 128), (144, 128)], [own, halo, packed], forces, scalars=0
    )
    (filtered,) = call(
        last_hop_kernel,
        [(192, 128)],
        [place, coefficients, spatial, two, one, fields, meet(two, chip), meet(two, across)],
        [(24,)],
        scalars=2,
    )
    return (
        new_links.reshape(links.shape),
        new_momenta.reshape(momenta.shape),
        filtered.reshape(vectors.shape),
    )


def solution(mesh):
    return jax.shard_map(
        functools.partial(body, pairs(mesh)),
        mesh=mesh,
        in_specs=(
            P(None, None, None, None, ("grp", "ta"), "xyz", None),
            P(None, None, None, None, ("grp", "ta"), "xyz", None),
            P("grp", None, None, None, "ta", "xyz", None),
            P(),
        ),
        out_specs=(
            P(None, None, None, None, ("grp", "ta"), "xyz", None),
            P(None, None, None, None, ("grp", "ta"), "xyz", None),
            P("grp", None, None, None, "ta", "xyz", None),
        ),
        check_vma=False,
    )
```

profile of v0, /device:TPU:112, one launch (start us, length us, event | category | flops | bytes accessed | tf_op | source)
XLA Modules:
  0.0 133.3 jit_solution(1964408196307695373)
XLA Ops:
  3.0 2.1 %all-gather = f32[36,8,128]{2,1,0:T(8,128)S(1)} all-gather(f32[18,8,128]{2,1,0:T(8,128)} %get-tuple-element.16.own_ref), channel_id=2, replica_groups={{0,1},{2,3},{4,5},{6,7},{8,9},{10,11},{12,13},{14,15},{16,17},{18,19},{..., dimensions={0}, use_global_device_ids=true | all-gather | bytes 221184 | tf_op jit(solution)/shard_map/all_gather | solution.py:497
  5.1 5.8 %all-gather.1 = f32[4,18,8,128]{3,2,1,0:T(8,128)S(1)} all-gather(f32[2,18,8,128]{3,2,1,0:T(8,128)S(1)} %bitcast.38), channel_id=3, replica_groups={{0,64},{128,192},{256,320},{384,448},{512,576},{640,704},{768,832},{896..., dimensions={0}, use_global_device_ids=true | all-gather | bytes 442368 | tf_op jit(solution)/shard_map/all_gather | solution.py:497
  10.9 3.1 %all-gather.2 = f32[4,2,18,8,128]{4,3,2,1,0:T(8,128)} all-gather(f32[2,2,18,8,128]{4,3,2,1,0:T(8,128)S(1)} %bitcast.40), channel_id=4, replica_groups={{0,1},{2,3},{4,5},{6,7},{8,9},{10,11},{12,13},{14,15},{16,17},{18,19},{..., dimensions={0}, use_global_device_ids=true | all-gather | bytes 884736 | tf_op jit(solution)/shard_map/all_gather | solution.py:497
  15.8 26.4 %all-gather.3 = f32[102,8,128]{2,1,0:T(8,128)} all-gather(f32[51,8,128]{2,1,0:T(8,128)} %shard_map.68), channel_id=5, replica_groups={{1,2},{3,4},{5,6},{7,8},{9,10},{11,12},{13,14},{15,16},{17,18},{19,20},..., dimensions={0}, use_global_device_ids=true | all-gather | bytes 626688 | tf_op jit(solution)/shard_map/all_gather | solution.py:497
  42.2 2.5 %shard_map.69 = (f32[4,18,8,128]{3,2,1,0:T(8,128)}, f32[8,8,128]{2,1,0:T(8,128)}) custom-call(s32[3]{0:T(128)} %pad_add_fusion.place_ref, f32[18,8,128]{2,1,0:T(8,128)} %get-tuple-element.16.own_ref, f32[8,8,128]{2,1,0:T(8,128)} %get-tuple-element.17.packed_ref, f32[2,18,8,128]{3,2,1,0:T(8,128)} %bitcast.39, f32[2,2,2,18,8,128]{5,4,3,2,1,0:T(8,128)} %bitcast.28, ...), custom_call_target="tpu_custom_call" | custom-call | tf_op jit(solution)/shard_map/pallas_call | solution.py:469
  44.7 2.1 %all-gather.4 = f32[16,8,128]{2,1,0:T(8,128)S(1)} all-gather(f32[8,8,128]{2,1,0:T(8,128)} %get-tuple-element.20.own_ref.packed_ref), channel_id=6, replica_groups={{0,1},{2,3},{4,5},{6,7},{8,9},{10,11},{12,13},{14,15},{16,17},{18,19},{..., dimensions={0}, use_global_device_ids=true | all-gather | bytes 98304 | tf_op jit(solution)/shard_map/all_gather | solution.py:497
  46.8 4.9 %all-gather.5 = f32[4,8,8,128]{3,2,1,0:T(8,128)S(1)} all-gather(f32[2,8,8,128]{3,2,1,0:T(8,128)S(1)} %bitcast.46), channel_id=7, replica_groups={{0,64},{128,192},{256,320},{384,448},{512,576},{640,704},{768,832},{896..., dimensions={0}, use_global_device_ids=true | all-gather | bytes 196608 | tf_op jit(solution)/shard_map/all_gather | solution.py:497
  51.7 2.9 %all-gather.6 = f32[4,2,8,8,128]{4,3,2,1,0:T(8,128)} all-gather(f32[2,2,8,8,128]{4,3,2,1,0:T(8,128)S(1)} %bitcast.50), channel_id=8, replica_groups={{0,1},{2,3},{4,5},{6,7},{8,9},{10,11},{12,13},{14,15},{16,17},{18,19},{..., dimensions={0}, use_global_device_ids=true | all-gather | bytes 393216 | tf_op jit(solution)/shard_map/all_gather | solution.py:497
  56.2 9.1 %all-gather.7 = f32[24,8,128]{2,1,0:T(8,128)} all-gather(f32[12,8,128]{2,1,0:T(8,128)} %shard_map.70), channel_id=9, replica_groups={{1,2},{3,4},{5,6},{7,8},{9,10},{11,12},{13,14},{15,16},{17,18},{19,20},..., dimensions={0}, use_global_device_ids=true | all-gather | bytes 147456 | tf_op jit(solution)/shard_map/all_gather | solution.py:497
  65.2 2.6 %shard_map.71 = (f32[18,8,128]{2,1,0:T(8,128)}, f32[4,18,8,128]{3,2,1,0:T(8,128)}, f32[8,8,128]{2,1,0:T(8,128)}) custom-call(s32[3]{0:T(128)} %pad_add_fusion.place_ref, f32[18,8,128]{2,1,0:T(8,128)} %get-tuple-element.16.own_ref, f32[4,18,8,128]{3,2,1,0:T(8,128)} %get-tuple-element.19.halo_ref, f32[8,8,128]{2,1,0:T(8,128)} %get-tuple-element.20.own_ref.packed_ref, ...), custom_call_target="tpu_custom_call" | custom-call | tf_op jit(solution)/shard_map/pallas_call | solution.py:469
  69.9 4.9 %all-gather.9 = f32[4,8,8,128]{3,2,1,0:T(8,128)S(1)} all-gather(f32[2,8,8,128]{3,2,1,0:T(8,128)S(1)} %bitcast.48), channel_id=11, replica_groups={{0,64},{128,192},{256,320},{384,448},{512,576},{640,704},{768,832},{896..., dimensions={0}, use_global_device_ids=true | all-gather | bytes 196608 | tf_op jit(solution)/shard_map/all_gather | solution.py:497
  74.8 2.9 %all-gather.10 = f32[4,2,8,8,128]{4,3,2,1,0:T(8,128)} all-gather(f32[2,2,8,8,128]{4,3,2,1,0:T(8,128)S(1)} %bitcast.51), channel_id=12, replica_groups={{0,1},{2,3},{4,5},{6,7},{8,9},{10,11},{12,13},{14,15},{16,17},{18,19},{..., dimensions={0}, use_global_device_ids=true | all-gather | bytes 393216 | tf_op jit(solution)/shard_map/all_gather | solution.py:497
  79.3 9.1 %all-gather.11 = f32[24,8,128]{2,1,0:T(8,128)} all-gather(f32[12,8,128]{2,1,0:T(8,128)} %shard_map.72), channel_id=13, replica_groups={{1,2},{3,4},{5,6},{7,8},{9,10},{11,12},{13,14},{15,16},{17,18},{19,20},..., dimensions={0}, use_global_device_ids=true | all-gather | bytes 147456 | tf_op jit(solution)/shard_map/all_gather | solution.py:497
  88.4 2.1 %shard_map.73 = (f32[18,8,128]{2,1,0:T(8,128)}, f32[4,18,8,128]{3,2,1,0:T(8,128)}, f32[18,8,128]{2,1,0:T(8,128)}) custom-call(s32[3]{0:T(128)} %pad_add_fusion.place_ref, f32[18,8,128]{2,1,0:T(8,128)} %get-tuple-element.21.own_ref, f32[4,18,8,128]{3,2,1,0:T(8,128)} %get-tuple-element.22.halo_ref, f32[8,8,128]{2,1,0:T(8,128)} %get-tuple-element.23.own_ref.packed_ref, ...), custom_call_target="tpu_custom_call" | custom-call | tf_op jit(solution)/shard_map/pallas_call | solution.py:469
  90.5 6.5 %all-gather.12 = f32[36,8,128]{2,1,0:T(8,128)} all-gather(f32[18,8,128]{2,1,0:T(8,128)} %get-tuple-element.28), channel_id=14, replica_groups={{0,512},{1,513},{2,514},{3,515},{4,516},{5,517},{6,518},{7,519},{8,520}..., dimensions={0}, use_global_device_ids=true | all-gather | bytes 221184 | tf_op jit(solution)/shard_map/all_gather | solution.py:497
  97.0 2.1 %all-gather.13 = f32[48,8,128]{2,1,0:T(8,128)} all-gather(f32[24,8,128]{2,1,0:T(8,128)S(1)} %copy-done), channel_id=15, replica_groups={{0,1},{2,3},{4,5},{6,7},{8,9},{10,11},{12,13},{14,15},{16,17},{18,19},{..., dimensions={0}, use_global_device_ids=true | all-gather | bytes 294912 | tf_op jit(solution)/shard_map/all_gather | solution.py:497
  99.1 2.2 %shard_map.75.field_ref.older_ref = f32[24,8,128]{2,1,0:T(8,128)} custom-call(s32[3]{0:T(128)} %pad_add_fusion.place_ref, f32[2,18,8,128]{3,2,1,0:T(8,128)} %bitcast.31, f32[24,8,128]{2,1,0:T(8,128)} %get-tuple-element.18.rest_0_.field_ref.older_ref.oldest_ref, f32[2,24,8,128]{3,2,1,0:T(8,128)} %bitcast.41, f32[2,51,8,128]{3,2,1,0:T(8,128)} %bitcast.30), custom_call_target="tpu_custom_call" | custom-call | tf_op jit(solution)/shard_map/pallas_call | solution.py:469
  101.3 3.5 %all-gather.14 = f32[48,8,128]{2,1,0:T(8,128)} all-gather(f32[24,8,128]{2,1,0:T(8,128)} %shard_map.75.field_ref.older_ref), channel_id=16, replica_groups={{0,1},{2,3},{4,5},{6,7},{8,9},{10,11},{12,13},{14,15},{16,17},{18,19},{..., dimensions={0}, use_global_device_ids=true | all-gather | bytes 294912 | tf_op jit(solution)/shard_map/all_gather | solution.py:497
  104.8 9.2 %all-gather.15 = f32[48,8,128]{2,1,0:T(8,128)} all-gather(f32[24,8,128]{2,1,0:T(8,128)S(1)} %copy-done.1), channel_id=17, replica_groups={{1,2},{3,4},{5,6},{7,8},{9,10},{11,12},{13,14},{15,16},{17,18},{19,20},..., dimensions={0}, use_global_device_ids=true | all-gather | bytes 294912 | tf_op jit(solution)/shard_map/all_gather | solution.py:497
  114.0 2.2 %shard_map.76.field_ref = f32[24,8,128]{2,1,0:T(8,128)} custom-call(s32[3]{0:T(128)} %pad_add_fusion.place_ref, f32[2,18,8,128]{3,2,1,0:T(8,128)} %bitcast.32, f32[24,8,128]{2,1,0:T(8,128)} %shard_map.75.field_ref.older_ref, f32[24,8,128]{2,1,0:T(8,128)} %get-tuple-element.18.rest_0_.field_ref.older_ref.oldest_ref, f32[2,24,8,128]{3,2,1,0:T(8,128)} %bitcast.44, ...), custom_call_target="tpu_custom_call" | custom-call | tf_op jit(solution)/shard_map/pallas_call | solution.py:469
  116.1 3.5 %all-gather.16 = f32[48,8,128]{2,1,0:T(8,128)} all-gather(f32[24,8,128]{2,1,0:T(8,128)} %shard_map.76.field_ref), channel_id=18, replica_groups={{0,1},{2,3},{4,5},{6,7},{8,9},{10,11},{12,13},{14,15},{16,17},{18,19},{..., dimensions={0}, use_global_device_ids=true | all-gather | bytes 294912 | tf_op jit(solution)/shard_map/all_gather | solution.py:497
  119.7 9.2 %all-gather.17 = f32[48,8,128]{2,1,0:T(8,128)} all-gather(f32[24,8,128]{2,1,0:T(8,128)S(1)} %copy-done.2), channel_id=19, replica_groups={{1,2},{3,4},{5,6},{7,8},{9,10},{11,12},{13,14},{15,16},{17,18},{19,20},..., dimensions={0}, use_global_device_ids=true | all-gather | bytes 294912 | tf_op jit(solution)/shard_map/all_gather | solution.py:497
  128.8 2.2 %shard_map.77 = f32[192,128]{1,0:T(8,128)} custom-call(s32[3]{0:T(128)} %pad_add_fusion.place_ref, f32[4]{0:T(128)} %coefficients_ref.1, f32[2,18,8,128]{3,2,1,0:T(8,128)} %bitcast.33, f32[24,8,128]{2,1,0:T(8,128)} %shard_map.76.field_ref, f32[24,8,128]{2,1,0:T(8,128)} %shard_map.75.field_ref.older_ref, ...), custom_call_target="tpu_custom_call" | custom-call | tf_op jit(solution)/shard_map/pallas_call | solution.py:469
  131.1 2.2 %shard_map.74 = (f32[144,128]{1,0:T(8,128)}, f32[144,128]{1,0:T(8,128)}) custom-call(f32[18,8,128]{2,1,0:T(8,128)} %get-tuple-element.24.own_ref, f32[4,18,8,128]{3,2,1,0:T(8,128)} %get-tuple-element.25.halo_ref, f32[8,8,128]{2,1,0:T(8,128)} %get-tuple-element.23.own_ref.packed_ref), custom_call_target="tpu_custom_call" | custom-call | tf_op jit(solution)/shard_map/pallas_call | solution.py:469
  (18 shorter events, 9.4 us)
Async XLA Ops:
  5.1 5.8 %copy-start.3 = (f32[36,8,128]{2,1,0:T(8,128)}, f32[36,8,128]{2,1,0:T(8,128)S(1)}, u32[]{:S(2)}) copy-start(f32[36,8,128]{2,1,0:T(8,128)S(1)} %all-gather) | copy-start | bytes 442372
  46.8 4.9 %copy-start.4 = (f32[16,8,128]{2,1,0:T(8,128)}, f32[16,8,128]{2,1,0:T(8,128)S(1)}, u32[]{:S(2)}) copy-start(f32[16,8,128]{2,1,0:T(8,128)S(1)} %all-gather.4) | copy-start | bytes 196612
  69.9 4.9 %copy-start.5 = (f32[16,8,128]{2,1,0:T(8,128)}, f32[16,8,128]{2,1,0:T(8,128)S(1)}, u32[]{:S(2)}) copy-start(f32[16,8,128]{2,1,0:T(8,128)S(1)} %all-gather.8) | copy-start | bytes 196612
  90.5 6.5 %copy-start = (f32[24,8,128]{2,1,0:T(8,128)S(1)}, f32[24,8,128]{2,1,0:T(8,128)}, u32[]{:S(2)}) copy-start(f32[24,8,128]{2,1,0:T(8,128)} %get-tuple-element.18.rest_0_.field_ref.older_ref.oldest_ref) | copy-start | bytes 294916
  101.3 3.6 %copy-start.1 = (f32[24,8,128]{2,1,0:T(8,128)S(1)}, f32[24,8,128]{2,1,0:T(8,128)}, u32[]{:S(2)}) copy-start(f32[24,8,128]{2,1,0:T(8,128)} %shard_map.75.field_ref.older_ref) | copy-start | bytes 294916
  116.1 3.6 %copy-start.2 = (f32[24,8,128]{2,1,0:T(8,128)S(1)}, f32[24,8,128]{2,1,0:T(8,128)}, u32[]{:S(2)}) copy-start(f32[24,8,128]{2,1,0:T(8,128)} %shard_map.76.field_ref) | copy-start | bytes 294916
where the time goes:
time: 134 us; the launch traced here: 133 us
  blocking collectives  109 us (81%)
  Pallas kernels  22.7 us (17%)
    all_gather x18, blocking collectives, meet(): return lax.all_gather(values, AXES, axis_index_groups=which)  109 us
    pallas_call x11, Pallas kernels, call(): pl.pallas_call(kernel, out_shape=outs, in_specs=[smem] * scalars + [vmem]...  22.7 us

commit v1 on v0

--- a/solution.py
+++ b/solution.py
@@ -472,6 +472,7 @@
         in_specs=[smem] * scalars + [vmem] * (len(inputs) - scalars),
         out_specs=[vmem] * len(outs),
         scratch_shapes=[pltpu.VMEM(shape + TILE, F32) for shape in scratch],
+        compiler_params=pltpu.CompilerParams(vmem_limit_bytes=8 << 20),
     )(*inputs)
     return result
 

time: 134 us -> 114 us (0.85)
  Pallas kernels: 22.7 us -> 10.2 us
  blocking collectives: 109 us -> 99.8 us
  local copies, waits for them, and re-layouts: 0.02 us -> 3.21 us
    pallas_call x11, Pallas kernels: 22.7 us -> 10.2 us  [call(): pl.pallas_call(kernel, out_shape=outs, in_specs=[smem] * scalars + [vmem]...]
    all_gather x18, blocking collectives: 109 us -> 99.8 us  [meet(): return lax.all_gather(values, AXES, axis_index_groups=which)]
    unnamed x12 -> x8, local copies, waits for them, and re-layouts: 0.02 us -> 3.21 us
where the time goes in v1:
time: 114 us
  blocking collectives  99.8 us (88%)
  Pallas kernels  10.2 us (9%)
  local copies, waits for them, and re-layouts  3.21 us (3%)
    all_gather x18, blocking collectives, meet(): return lax.all_gather(values, AXES, axis_index_groups=which)  99.8 us
    pallas_call x11, Pallas kernels, call(): pl.pallas_call(kernel, out_shape=outs, in_specs=[smem] * scalars + [vmem]...  10.2 us
    unnamed x8, local copies, waits for them, and re-layouts  3.21 us

profile of v1, /device:TPU:112, one launch (start us, length us, event | category | flops | bytes accessed | tf_op | source)
XLA Modules:
  0.0 114.0 jit_solution(6950371880850619724)
XLA Ops:
  1.5 0.9 copy-done
  2.4 0.9 copy-done.2
  3.9 1.9 %all-gather = f32[36,8,128]{2,1,0:T(8,128)S(1)} all-gather(f32[18,8,128]{2,1,0:T(8,128)S(1)} %get-tuple-element.16.own_ref), channel_id=2, replica_groups={{0,1},{2,3},{4,5},{6,7},{8,9},{10,11},{12,13},{14,15},{16,17},{18,19},{..., dimensions={0}, use_global_device_ids=true | all-gather | bytes 221184 | tf_op jit(solution)/shard_map/all_gather | solution.py:498
  5.8 5.8 %all-gather.1 = f32[4,18,8,128]{3,2,1,0:T(8,128)S(1)} all-gather(f32[2,18,8,128]{3,2,1,0:T(8,128)S(1)} %bitcast.38), channel_id=3, replica_groups={{0,64},{128,192},{256,320},{384,448},{512,576},{640,704},{768,832},{896..., dimensions={0}, use_global_device_ids=true | all-gather | bytes 442368 | tf_op jit(solution)/shard_map/all_gather | solution.py:498
  11.6 3.0 %all-gather.2 = f32[4,2,18,8,128]{4,3,2,1,0:T(8,128)S(1)} all-gather(f32[2,2,18,8,128]{4,3,2,1,0:T(8,128)S(1)} %bitcast.54), channel_id=4, replica_groups={{0,1},{2,3},{4,5},{6,7},{8,9},{10,11},{12,13},{14,15},{16,17},{18,19},{..., dimensions={0}, use_global_device_ids=true | all-gather | bytes 884736 | tf_op jit(solution)/shard_map/all_gather | solution.py:498
  15.1 22.4 %all-gather.3 = f32[102,8,128]{2,1,0:T(8,128)S(1)} all-gather(f32[51,8,128]{2,1,0:T(8,128)S(1)} %shard_map.68), channel_id=5, replica_groups={{1,2},{3,4},{5,6},{7,8},{9,10},{11,12},{13,14},{15,16},{17,18},{19,20},..., dimensions={0}, use_global_device_ids=true | all-gather | bytes 626688 | tf_op jit(solution)/shard_map/all_gather | solution.py:498
  37.5 1.2 %shard_map.69 = (f32[4,18,8,128]{3,2,1,0:T(8,128)S(1)}, f32[8,8,128]{2,1,0:T(8,128)S(1)}) custom-call(s32[3]{0:T(128)S(1)} %pad_add_fusion.place_ref, f32[18,8,128]{2,1,0:T(8,128)S(1)} %get-tuple-element.16.own_ref, f32[8,8,128]{2,1,0:T(8,128)S(1)} %get-tuple-element.17.packed_ref, f32[2,18,8,128]{3,2,1,0:T(8,128)S(1)} %bitcast.39, ...), custom_call_target="tpu_custom_call" | custom-call | tf_op jit(solution)/shard_map/pallas_call | solution.py:469
  38.7 1.9 %all-gather.4 = f32[16,8,128]{2,1,0:T(8,128)S(1)} all-gather(f32[8,8,128]{2,1,0:T(8,128)S(1)} %get-tuple-element.20.own_ref.packed_ref), channel_id=6, replica_groups={{0,1},{2,3},{4,5},{6,7},{8,9},{10,11},{12,13},{14,15},{16,17},{18,19},{..., dimensions={0}, use_global_device_ids=true | all-gather | bytes 98304 | tf_op jit(solution)/shard_map/all_gather | solution.py:498
  40.5 4.9 %all-gather.5 = f32[4,8,8,128]{3,2,1,0:T(8,128)S(1)} all-gather(f32[2,8,8,128]{3,2,1,0:T(8,128)S(1)} %bitcast.45), channel_id=7, replica_groups={{0,64},{128,192},{256,320},{384,448},{512,576},{640,704},{768,832},{896..., dimensions={0}, use_global_device_ids=true | all-gather | bytes 196608 | tf_op jit(solution)/shard_map/all_gather | solution.py:498
  45.5 2.7 %all-gather.6 = f32[4,2,8,8,128]{4,3,2,1,0:T(8,128)S(1)} all-gather(f32[2,2,8,8,128]{4,3,2,1,0:T(8,128)S(1)} %bitcast.55), channel_id=8, replica_groups={{0,1},{2,3},{4,5},{6,7},{8,9},{10,11},{12,13},{14,15},{16,17},{18,19},{..., dimensions={0}, use_global_device_ids=true | all-gather | bytes 393216 | tf_op jit(solution)/shard_map/all_gather | solution.py:498
  48.8 8.4 %all-gather.7 = f32[24,8,128]{2,1,0:T(8,128)S(1)} all-gather(f32[12,8,128]{2,1,0:T(8,128)S(1)} %shard_map.70), channel_id=9, replica_groups={{1,2},{3,4},{5,6},{7,8},{9,10},{11,12},{13,14},{15,16},{17,18},{19,20},..., dimensions={0}, use_global_device_ids=true | all-gather | bytes 147456 | tf_op jit(solution)/shard_map/all_gather | solution.py:498
  57.2 1.4 %shard_map.71 = (f32[18,8,128]{2,1,0:T(8,128)S(1)}, f32[4,18,8,128]{3,2,1,0:T(8,128)S(1)}, f32[8,8,128]{2,1,0:T(8,128)S(1)}) custom-call(s32[3]{0:T(128)S(1)} %pad_add_fusion.place_ref, f32[18,8,128]{2,1,0:T(8,128)S(1)} %get-tuple-element.16.own_ref, f32[4,18,8,128]{3,2,1,0:T(8,128)S(1)} %get-tuple-element.19.halo_ref, ...), custom_call_target="tpu_custom_call" | custom-call | tf_op jit(solution)/shard_map/pallas_call | solution.py:469
  58.6 1.9 %all-gather.8 = f32[16,8,128]{2,1,0:T(8,128)S(1)} all-gather(f32[8,8,128]{2,1,0:T(8,128)S(1)} %get-tuple-element.23.own_ref.packed_ref), channel_id=10, replica_groups={{0,1},{2,3},{4,5},{6,7},{8,9},{10,11},{12,13},{14,15},{16,17},{18,19},{..., dimensions={0}, use_global_device_ids=true | all-gather | bytes 98304 | tf_op jit(solution)/shard_map/all_gather | solution.py:498
  60.4 4.9 %all-gather.9 = f32[4,8,8,128]{3,2,1,0:T(8,128)S(1)} all-gather(f32[2,8,8,128]{3,2,1,0:T(8,128)S(1)} %bitcast.47), channel_id=11, replica_groups={{0,64},{128,192},{256,320},{384,448},{512,576},{640,704},{768,832},{896..., dimensions={0}, use_global_device_ids=true | all-gather | bytes 196608 | tf_op jit(solution)/shard_map/all_gather | solution.py:498
  65.3 2.7 %all-gather.10 = f32[4,2,8,8,128]{4,3,2,1,0:T(8,128)S(1)} all-gather(f32[2,2,8,8,128]{4,3,2,1,0:T(8,128)S(1)} %bitcast.56), channel_id=12, replica_groups={{0,1},{2,3},{4,5},{6,7},{8,9},{10,11},{12,13},{14,15},{16,17},{18,19},{..., dimensions={0}, use_global_device_ids=true | all-gather | bytes 393216 | tf_op jit(solution)/shard_map/all_gather | solution.py:498
  68.6 8.4 %all-gather.11 = f32[24,8,128]{2,1,0:T(8,128)S(1)} all-gather(f32[12,8,128]{2,1,0:T(8,128)S(1)} %shard_map.72), channel_id=13, replica_groups={{1,2},{3,4},{5,6},{7,8},{9,10},{11,12},{13,14},{15,16},{17,18},{19,20},..., dimensions={0}, use_global_device_ids=true | all-gather | bytes 147456 | tf_op jit(solution)/shard_map/all_gather | solution.py:498
  77.9 5.2 %all-gather.12 = f32[36,8,128]{2,1,0:T(8,128)S(1)} all-gather(f32[18,8,128]{2,1,0:T(8,128)S(1)} %get-tuple-element.28), channel_id=14, replica_groups={{0,512},{1,513},{2,514},{3,515},{4,516},{5,517},{6,518},{7,519},{8,520}..., dimensions={0}, use_global_device_ids=true | all-gather | bytes 221184 | tf_op jit(solution)/shard_map/all_gather | solution.py:498
  83.1 1.9 %all-gather.13 = f32[48,8,128]{2,1,0:T(8,128)S(1)} all-gather(f32[24,8,128]{2,1,0:T(8,128)S(1)} %get-tuple-element.18.rest_0_.field_ref.older_ref.oldest_ref), channel_id=15, replica_groups={{0,1},{2,3},{4,5},{6,7},{8,9},{10,11},{12,13},{14,15},{16,17},{18,19},{..., dimensions={0}, use_global_device_ids=true | all-gather | bytes 294912 | tf_op jit(solution)/shard_map/all_gather | solution.py:498
  85.9 1.9 %all-gather.14 = f32[48,8,128]{2,1,0:T(8,128)S(1)} all-gather(f32[24,8,128]{2,1,0:T(8,128)S(1)} %shard_map.75.field_ref.older_ref), channel_id=16, replica_groups={{0,1},{2,3},{4,5},{6,7},{8,9},{10,11},{12,13},{14,15},{16,17},{18,19},{..., dimensions={0}, use_global_device_ids=true | all-gather | bytes 294912 | tf_op jit(solution)/shard_map/all_gather | solution.py:498
  87.8 10.1 %all-gather.15 = f32[48,8,128]{2,1,0:T(8,128)S(1)} all-gather(f32[24,8,128]{2,1,0:T(8,128)S(1)} %shard_map.75.field_ref.older_ref), channel_id=17, replica_groups={{1,2},{3,4},{5,6},{7,8},{9,10},{11,12},{13,14},{15,16},{17,18},{19,20},..., dimensions={0}, use_global_device_ids=true | all-gather | bytes 294912 | tf_op jit(solution)/shard_map/all_gather | solution.py:498
  98.8 1.9 %all-gather.16 = f32[48,8,128]{2,1,0:T(8,128)S(1)} all-gather(f32[24,8,128]{2,1,0:T(8,128)S(1)} %shard_map.76.field_ref), channel_id=18, replica_groups={{0,1},{2,3},{4,5},{6,7},{8,9},{10,11},{12,13},{14,15},{16,17},{18,19},{..., dimensions={0}, use_global_device_ids=true | all-gather | bytes 294912 | tf_op jit(solution)/shard_map/all_gather | solution.py:498
  100.7 9.8 %all-gather.17 = f32[48,8,128]{2,1,0:T(8,128)S(1)} all-gather(f32[24,8,128]{2,1,0:T(8,128)S(1)} %shard_map.76.field_ref), channel_id=19, replica_groups={{1,2},{3,4},{5,6},{7,8},{9,10},{11,12},{13,14},{15,16},{17,18},{19,20},..., dimensions={0}, use_global_device_ids=true | all-gather | bytes 294912 | tf_op jit(solution)/shard_map/all_gather | solution.py:498
  111.2 1.5 %shard_map.77 = f32[192,128]{1,0:T(8,128)} custom-call(s32[3]{0:T(128)S(1)} %pad_add_fusion.place_ref, f32[4]{0:T(128)S(1)} %copy-done.3, f32[2,18,8,128]{3,2,1,0:T(8,128)S(1)} %bitcast.33, f32[24,8,128]{2,1,0:T(8,128)S(1)} %shard_map.76.field_ref, f32[24,8,128]{2,1,0:T(8,128)S(1)} %shard_map.75.field_ref.older_ref, ...), custom_call_target="tpu_custom_call" | custom-call | tf_op jit(solution)/shard_map/pallas_call | solution.py:469
  112.7 1.3 %shard_map.74 = (f32[144,128]{1,0:T(8,128)}, f32[144,128]{1,0:T(8,128)}) custom-call(f32[18,8,128]{2,1,0:T(8,128)S(1)} %get-tuple-element.24.own_ref, f32[4,18,8,128]{3,2,1,0:T(8,128)S(1)} %get-tuple-element.25.halo_ref, f32[8,8,128]{2,1,0:T(8,128)S(1)} %get-tuple-element.23.own_ref.packed_ref), custom_call_target="tpu_custom_call" | custom-call | tf_op jit(solution)/shard_map/pallas_call | solution.py:469
  (14 shorter events, 6.3 us)
Async XLA Ops:
  0.6 0.9 copy-start.1
  1.5 0.9 copy-start
  2.4 0.9 copy-start.2
  110.5 0.7 copy-start.3

commit v2 on v1

--- a/solution.py
+++ b/solution.py
@@ -253,40 +253,48 @@
     return out
 
 
-def halo_entries(place, count, pair_ref, sides_ref, across_ref):
+def completed(entry):
+    tiles = [entry(c) for c in range(12)]
+    a = [(tiles[2 * j], tiles[2 * j + 1]) for j in range(3)]
+    b = [(tiles[6 + 2 * j], tiles[7 + 2 * j]) for j in range(3)]
+    for j in range(3):
+        p, q = (j + 1) % 3, (j + 2) % 3
+        real = (a[p][0] * b[q][0] - a[p][1] * b[q][1]) - (a[q][0] * b[p][0] - a[q][1] * b[p][1])
+        imag = (a[p][0] * b[q][1] + a[p][1] * b[q][0]) - (a[q][0] * b[p][1] + a[q][1] * b[p][0])
+        tiles += [real, -imag]
+    return tiles
+
+
+def paired(even, odd):
     row, _ = iotas()
-    odd_time, odd_space = place
-    first = odd_space == 0
-
-    def corner(c):
-        value = across_ref[odd_space, count + c // 2]
-        return roll(value, 4, 0) if c % 2 else value
-
-    def entry(h, c):
-        if h == 0:
-            value = sides_ref[odd_time, 1, odd_space, c]
-            extra = jnp.where(first, corner(c), sides_ref[odd_time, 1, 1 - odd_space, c])
-            return jnp.where(row < 2, roll(extra, -2, 0), value)
-        if h == 1:
-            return sides_ref[1 - odd_time, 0, odd_space, c]
-        near, far = pair_ref[1 - odd_space, c], across_ref[odd_space, c]
-        if h == 2:
-            value = jnp.where(first, near, far)
-            extra = jnp.where(first, sides_ref[1 - odd_time, 0, 1 - odd_space, c], corner(c))
-            return jnp.where(row // 2 == 1, roll(extra, 2, 0), value)
-        return jnp.where(first, far, near)
-
-    return entry
-
-
-def split_kernel(place_ref, links_ref, momenta_ref, vectors_ref, own_ref, packed_ref, fields_ref):
+    return jnp.where(row < 4, even, roll(odd, 4, 0))
+
+
+def unpaired(tile, c):
+    return roll(tile, 4, 0) if c % 2 else tile
+
+
+PACKED = (1, 9, 2, 3, 4, 5, 10, 11)
+
+
+def split_kernel(place_ref, links_hbm, momenta_hbm, vectors_hbm, own_ref, packed_ref, send_ref, links_ref, momenta_ref, vectors_ref, sems):
     half = place_ref[2]
+    copies = [
+        pltpu.make_async_copy(source, target, sems.at[i])
+        for i, (source, target) in enumerate(
+            ((links_hbm, links_ref), (vectors_hbm, vectors_ref), (momenta_hbm, momenta_ref))
+        )
+    ]
+    for copy in copies:
+        copy.start()
+    copies[0].wait()
     for c in range(18):
         for d in range(4):
-            own_ref[c, 2 * d : 2 * d + 2, :] = links_ref[d * 36 + 2 * c : d * 36 + 2 * c + 2, :]
-    for slot, c in enumerate(PACKED):
-        for d in range(4):
-            packed_ref[slot, 2 * d : 2 * d + 2, :] = momenta_ref[d * 36 + 2 * c : d * 36 + 2 * c + 2, :]
+            value = links_ref[d * 36 + 2 * c : d * 36 + 2 * c + 2, :]
+            own_ref[c, 2 * d : 2 * d + 2, :] = value
+            if c < 12:
+                send_ref[c, 2 * d : 2 * d + 2, :] = value
+    copies[1].wait()
     for c in range(6):
         for block in range(2):
             tiles = []
@@ -295,65 +303,184 @@
                     vectors_ref[pl.ds(block * 96 + c * 4 + h * 2 + side, 4, stride=24), :] for side in range(2)
                 ]
                 tiles.append(jnp.concatenate(parts, axis=0))
-            fields_ref[c * 4 + block] = jnp.where(half == 0, tiles[0], tiles[1])
-            fields_ref[c * 4 + 2 + block] = jnp.where(half == 0, tiles[1], tiles[0])
-
-
-PACKED = (1, 9, 2, 3, 4, 5, 10, 11)
-
-
-def bundle_kernel(count, extra, place_ref, own_ref, sides_ref, *rest):
+            send_ref[12 + c * 4 + block] = jnp.where(half == 0, tiles[0], tiles[1])
+            send_ref[12 + c * 4 + 2 + block] = jnp.where(half == 0, tiles[1], tiles[0])
+    copies[2].wait()
+    for slot, c in enumerate(PACKED):
+        for d in range(4):
+            packed_ref[slot, 2 * d : 2 * d + 2, :] = momenta_ref[d * 36 + 2 * c : d * 36 + 2 * c + 2, :]
+
+
+def first_bundle_kernel(place_ref, send_ref, packed_ref, near_ref, sides_ref, out_ref):
     row, _ = iotas()
     odd_time, odd_space = place_ref[0], place_ref[1]
-    out_ref = rest[-1]
-
-    def corner(c):
+    first = odd_space == 0
+    for c in range(12):
         ahead = sides_ref[odd_time, 1, odd_space, c]
-        behind = sides_ref[1 - odd_time, 0, odd_space, c]
-        return jnp.where(row < 2, behind, ahead)
-
-    for c in range(count):
-        out_ref[c] = own_ref[c]
-    for pair in range(count // 2):
-        out_ref[count + pair] = jnp.where(row < 4, corner(2 * pair), roll(corner(2 * pair + 1), 4, 0))
-    for c in range(extra):
-        out_ref[count + count // 2 + c] = rest[0][c]
-
-
-def first_kernel(place_ref, own_ref, packed_ref, pair_ref, sides_ref, across_ref, halo_ref, next_ref, forward, work):
-    entry = halo_entries((place_ref[0], place_ref[1]), 18, pair_ref, sides_ref, across_ref)
-    for h in range(4):
-        for c in range(18):
-            halo_ref[h, c] = entry(h, c)
-    kick = force(lambda c: own_ref[c], lambda h, c: halo_ref[h, c], forward, work)
+        ahead_other = sides_ref[odd_time, 1, 1 - odd_space, c]
+        behind_other = sides_ref[1 - odd_time, 0, 1 - odd_space, c]
+        partner = near_ref[1 - odd_space, c]
+        out_ref[c] = send_ref[c]
+        out_ref[12 + c] = jnp.where(row < 2, roll(ahead_other, -2, 0), ahead)
+        out_ref[24 + c] = sides_ref[1 - odd_time, 0, odd_space, c]
+        out_ref[36 + c] = jnp.where(first & (row // 2 == 1), roll(behind_other, 2, 0), partner)
     for c in range(8):
-        next_ref[c] = packed_ref[c] - (0.5 * time_step) * kick[c]
-
-
-def drift(place_ref, own_ref, halo_ref, packed_ref, pair_ref, sides_ref, across_ref, new_own_ref, new_halo_ref):
-    entry = halo_entries((place_ref[0], place_ref[1]), 8, pair_ref, sides_ref, across_ref)
-    store_matrix(new_own_ref, (), updated(lambda c: packed_ref[c], lambda c: own_ref[c]))
+        out_ref[48 + c] = packed_ref[c]
+    for c in range(24):
+        out_ref[56 + c] = send_ref[12 + c]
+        out_ref[80 + c] = near_ref[1 - odd_space, 12 + c]
+
+
+def first_kernel(
+    place_ref, own_ref, packed_ref, near_ref, sides_ref, across_ref,
+    halo_ref, send_ref, far_packed_ref, forward, work, far_own, far_halo,
+):
+    row, _ = iotas()
+    odd_time, odd_space = place_ref[0], place_ref[1]
+    first = odd_space == 0
+    x_row = row // 2 == 1
+
+    def ahead(c):
+        return sides_ref[odd_time, 1, odd_space, c]
+
+    def behind(c):
+        return sides_ref[1 - odd_time, 0, odd_space, c]
+
+    def ahead_other(c):
+        return sides_ref[odd_time, 1, 1 - odd_space, c]
+
+    def behind_other(c):
+        return sides_ref[1 - odd_time, 0, 1 - odd_space, c]
+
+    def near(c):
+        return near_ref[1 - odd_space, c]
+
+    def far(group, c):
+        return across_ref[odd_space, group * 12 + c]
+
+    def own(c):
+        return own_ref[c]
+
+    def put(ref, lead, entry):
+        for c, tile in enumerate(completed(entry)):
+            ref[lead + (c,)] = tile
+
+    put(halo_ref, (0,), lambda c: jnp.where(row < 2, roll(jnp.where(first, far(1, c), ahead_other(c)), -2, 0), ahead(c)))
+    put(halo_ref, (1,), behind)
+    put(
+        halo_ref,
+        (2,),
+        lambda c: jnp.where(
+            x_row,
+            roll(jnp.where(first, behind_other(c), far(2, c)), 2, 0),
+            jnp.where(first, near(c), far(0, c)),
+        ),
+    )
+    put(halo_ref, (3,), lambda c: jnp.where(first, far(0, c), near(c)))
+    put(far_own, (), lambda c: far(0, c))
+    put(far_halo, (0,), lambda c: jnp.where((row < 2) & (odd_space == 1), roll(ahead(c), -2, 0), far(1, c)))
+    put(far_halo, (1,), lambda c: far(2, c))
+    put(far_halo, (2,), lambda c: jnp.where(first, jnp.where(x_row, roll(behind(c), 2, 0), own(c)), far(3, c)))
+    put(far_halo, (3,), lambda c: jnp.where(first, far(3, c), own(c)))
+    kick = force(lambda c: far_own[c], lambda h, c: far_halo[h, c], forward, work)
+    moved = [far(4, c) - (0.5 * time_step) * kick[c] for c in range(8)]
+    for c in range(8):
+        far_packed_ref[c] = moved[c]
+    for pair in range(4):
+        send_ref[8 + pair] = paired(moved[2 * pair], moved[2 * pair + 1])
+    kick = force(own, lambda h, c: halo_ref[h, c], forward, work)
+    for c in range(8):
+        send_ref[c] = packed_ref[c] - (0.5 * time_step) * kick[c]
+
+
+def drift(own_ref, halo_ref, packed, entry, new_own_ref, new_halo_ref):
+    store_matrix(new_own_ref, (), updated(packed, lambda c: own_ref[c]))
     for h in range(4):
         store_matrix(new_halo_ref, (h,), updated(lambda c: entry(h, c), lambda c: halo_ref[h, c]))
 
 
 def middle_kernel(
-    place_ref, own_ref, halo_ref, packed_ref, pair_ref, sides_ref, across_ref,
+    place_ref, own_ref, halo_ref, send_ref, far_packed_ref, near_ref, sides_ref,
     new_own_ref, new_halo_ref, next_ref, forward, work,
 ):
-    drift(place_ref, own_ref, halo_ref, packed_ref, pair_ref, sides_ref, across_ref, new_own_ref, new_halo_ref)
+    row, _ = iotas()
+    odd_time, odd_space = place_ref[0], place_ref[1]
+    first = odd_space == 0
+
+    def entry(h, c):
+        if h == 0:
+            main, corner = sides_ref[odd_time, 1, 0, c], unpaired(sides_ref[odd_time, 1, 0, 8 + c // 2], c)
+            extra = jnp.where(first, corner, main)
+            return jnp.where(row < 2, roll(extra, -2, 0), sides_ref[odd_time, 1, odd_space, c])
+        if h == 1:
+            return sides_ref[1 - odd_time, 0, odd_space, c]
+        near, far = near_ref[1 - odd_space, c], far_packed_ref[c]
+        if h == 2:
+            main, corner = sides_ref[1 - odd_time, 0, 1, c], unpaired(sides_ref[1 - odd_time, 0, 1, 8 + c // 2], c)
+            extra = jnp.where(first, main, corner)
+            return jnp.where(row // 2 == 1, roll(extra, 2, 0), jnp.where(first, near, far))
+        return jnp.where(first, far, near)
+
+    drift(own_ref, halo_ref, lambda c: send_ref[c], entry, new_own_ref, new_halo_ref)
     kick = force(lambda c: new_own_ref[c], lambda h, c: new_halo_ref[h, c], forward, work)
     for c in range(8):
-        next_ref[c] = packed_ref[c] - time_step * kick[c]
+        next_ref[c] = send_ref[c] - time_step * kick[c]
+
+
+def last_bundle_kernel(place_ref, own_ref, halo_ref, packed_ref, near_ref, sides_ref, out_ref):
+    row, _ = iotas()
+    odd_time, odd_space = place_ref[0], place_ref[1]
+    first = odd_space == 0
+
+    def corner(c):
+        return jnp.where(row < 2, sides_ref[1 - odd_time, 0, odd_space, c], sides_ref[odd_time, 1, odd_space, c])
+
+    for c in range(8):
+        out_ref[c] = packed_ref[c]
+    for pair in range(4):
+        out_ref[8 + pair] = paired(corner(2 * pair), corner(2 * pair + 1))
+    even = updated(
+        lambda c: jnp.where(first, packed_ref[c], near_ref[1 - odd_space, c]),
+        lambda c: jnp.where(first, own_ref[c], halo_ref[3, c]),
+    )
+    for pair in range(9):
+        i, j = pair // 3, pair % 3
+        out_ref[12 + pair] = paired(even[i][j][0], even[i][j][1])
 
 
 def last_drift_kernel(
-    place_ref, own_ref, halo_ref, packed_ref, pair_ref, sides_ref, across_ref, new_own_ref, new_halo_ref, spatial_ref
+    place_ref, own_ref, halo_ref, packed_ref, near_ref, sides_ref, across_ref,
+    new_own_ref, new_halo_ref, spatial_ref,
 ):
-    drift(place_ref, own_ref, halo_ref, packed_ref, pair_ref, sides_ref, across_ref, new_own_ref, new_halo_ref)
     row, _ = iotas()
+    odd_time, odd_space = place_ref[0], place_ref[1]
+    first = odd_space == 0
+    x_row = row // 2 == 1
+
+    def entry(h, c):
+        if h == 0:
+            corner = unpaired(across_ref[odd_space, 8 + c // 2], c)
+            extra = jnp.where(first, corner, sides_ref[odd_time, 1, 1 - odd_space, c])
+            return jnp.where(row < 2, roll(extra, -2, 0), sides_ref[odd_time, 1, odd_space, c])
+        if h == 1:
+            return sides_ref[1 - odd_time, 0, odd_space, c]
+        near, far = near_ref[1 - odd_space, c], across_ref[odd_space, c]
+        if h == 2:
+            corner = unpaired(across_ref[odd_space, 8 + c // 2], c)
+            extra = jnp.where(first, sides_ref[1 - odd_time, 0, 1 - odd_space, c], corner)
+            return jnp.where(x_row, roll(extra, 2, 0), jnp.where(first, near, far))
+        return jnp.where(first, far, near)
+
+    drift(own_ref, halo_ref, lambda c: packed_ref[c], entry, new_own_ref, new_halo_ref)
     for c in range(18):
-        spatial_ref[c] = jnp.where(row < 2, roll(new_halo_ref[3, c], -2, 0), new_own_ref[c])
+        own, right, left = new_own_ref[c], new_halo_ref[2, c], new_halo_ref[3, c]
+        even = unpaired(across_ref[odd_space, 12 + c // 2], c)
+        spatial_ref[0, c] = jnp.where(row < 2, roll(left, -2, 0), own)
+        spatial_ref[1, c] = jnp.where(
+            first,
+            jnp.where(row < 2, roll(even, -2, 0), left),
+            jnp.where(row < 2, roll(own, -2, 0), jnp.where(x_row, even, right)),
+        )
 
 
 def last_force_kernel(own_ref, halo_ref, packed_ref, links_ref, momenta_ref, forward, work):
@@ -369,24 +496,20 @@
             momenta_ref[d * 36 + 2 * c : d * 36 + 2 * c + 2, :] = full[c][2 * d : 2 * d + 2, :]
 
 
-def hopping(place_ref, spatial_ref, field_ref, near_ref, across_ref, offset, emit):
+def hopping(half, links, field, ahead, behind, emit):
     row, lane = iotas()
-    odd_space, half = place_ref[1], place_ref[2]
-    first = odd_space == 0
     for side in range(2):
         owner = half if side == 0 else 1 - half
 
         def link(d, c):
-            low = jnp.broadcast_to(spatial_ref[owner, c, 2 * d : 2 * d + 1, :], TILE)
-            high = jnp.broadcast_to(spatial_ref[owner, c, 2 * d + 1 : 2 * d + 2, :], TILE)
+            low = jnp.broadcast_to(links(owner, c, slice(2 * d, 2 * d + 1)), TILE)
+            high = jnp.broadcast_to(links(owner, c, slice(2 * d + 1, 2 * d + 2)), TILE)
             return jnp.where(row < 4, low, high)
 
         totals = {}
         for d in range(4):
             matrix = load_matrix(lambda c: link(d, c))
             for block in range(2):
-                def tile(c):
-                    return c * 4 + side * 2 + block
 
                 def times(vector, dagger):
                     out = []
@@ -404,21 +527,20 @@
                         out += [real, imag]
                     return out
 
-                if d < 2:
-                    vector = []
-                    for c in range(6):
-                        near, far = near_ref[1 - odd_space, tile(c)], across_ref[odd_space, offset + tile(c)]
-                        vector.append(jnp.where(first, near, far) if d == 1 else jnp.where(first, far, near))
-                    parts = [times(vector, d == 0)]
+                tiles = [c * 4 + side * 2 + block for c in range(6)]
+                if d == 0:
+                    parts = [times([behind(tile) for tile in tiles], True)]
+                elif d == 1:
+                    parts = [times([ahead(tile) for tile in tiles], False)]
                 else:
-                    values = [field_ref[tile(c)] for c in range(6)]
+                    values = [field(tile) for tile in tiles]
                     back = times(values, True)
                     if d == 2:
-                        ahead = times([vector_shift_y(v, 1, lane) for v in values], False)
-                        parts = [ahead, [vector_shift_y(v, -1, lane) for v in back]]
+                        front = times([vector_shift_y(v, 1, lane) for v in values], False)
+                        parts = [front, [vector_shift_y(v, -1, lane) for v in back]]
                     else:
-                        ahead = times([shift_z(v, 1, lane) for v in values], False)
-                        parts = [ahead, [shift_z(v, -1, lane) for v in back]]
+                        front = times([shift_z(v, 1, lane) for v in values], False)
+                        parts = [front, [shift_z(v, -1, lane) for v in back]]
                 for part in parts:
                     for c in range(6):
                         old = totals.get((block, c))
@@ -428,31 +550,91 @@
                 emit(c * 4 + side * 2 + block, totals[block, c] * (-1.0 / 6.0))
 
 
-def first_hop_kernel(offset, place_ref, spatial_ref, field_ref, near_ref, across_ref, out_ref):
+def first_hop_kernel(place_ref, spatial_ref, field_ref, near_ref, across_ref, out_ref, far_out_ref):
+    odd_space, half = place_ref[1], place_ref[2]
+    first = odd_space == 0
+
+    def own(tile):
+        return field_ref[12 + tile]
+
+    def near(tile):
+        return near_ref[1 - odd_space, 12 + tile]
+
+    def far(tile):
+        return across_ref[odd_space, 56 + tile]
+
+    def farther(tile):
+        return across_ref[odd_space, 80 + tile]
+
+    def put(ref):
+        def emit(tile, value):
+            ref[tile] = value
+
+        return emit
+
+    hopping(
+        half,
+        lambda owner, c, rows: spatial_ref[owner, 0, c, rows, :],
+        own,
+        lambda tile: jnp.where(first, near(tile), far(tile)),
+        lambda tile: jnp.where(first, far(tile), near(tile)),
+        put(out_ref),
+    )
+    hopping(
+        half,
+        lambda owner, c, rows: spatial_ref[owner, 1, c, rows, :],
+        far,
+        lambda tile: jnp.where(first, own(tile), farther(tile)),
+        lambda tile: jnp.where(first, farther(tile), own(tile)),
+        put(far_out_ref),
+    )
+
+
+def second_hop_kernel(place_ref, spatial_ref, field_ref, older_ref, near_ref, far_ref, out_ref):
+    odd_space, half = place_ref[1], place_ref[2]
+    first = odd_space == 0
+
+    def near(tile):
+        return near_ref[1 - odd_space, tile]
+
     def emit(tile, value):
-        out_ref[tile] = value
-
-    hopping(place_ref, spatial_ref, field_ref, near_ref, across_ref, offset, emit)
-
-
-def next_hop_kernel(place_ref, spatial_ref, field_ref, older_ref, near_ref, across_ref, out_ref):
-    def emit(tile, value):
-        out_ref[tile] = 2.0 * value - older_ref[tile]
-
-    hopping(place_ref, spatial_ref, field_ref, near_ref, across_ref, 0, emit)
+        out_ref[tile] = 2.0 * value - older_ref[12 + tile]
+
+    hopping(
+        half,
+        lambda owner, c, rows: spatial_ref[owner, 0, c, rows, :],
+        lambda tile: field_ref[tile],
+        lambda tile: jnp.where(first, near(tile), far_ref[tile]),
+        lambda tile: jnp.where(first, far_ref[tile], near(tile)),
+        emit,
+    )
 
 
 def last_hop_kernel(
     place_ref, coefficients_ref, spatial_ref, field_ref, older_ref, oldest_ref, near_ref, across_ref, out_ref, work
 ):
-    half = place_ref[2]
+    odd_space, half = place_ref[1], place_ref[2]
+    first = odd_space == 0
+
+    def near(tile):
+        return near_ref[1 - odd_space, tile]
+
+    def far(tile):
+        return across_ref[odd_space, tile]
 
     def emit(tile, value):
         newest = 2.0 * value - older_ref[tile]
-        total = coefficients_ref[0] * oldest_ref[tile] + coefficients_ref[1] * older_ref[tile]
+        total = coefficients_ref[0] * oldest_ref[12 + tile] + coefficients_ref[1] * older_ref[tile]
         work[tile] = total + coefficients_ref[2] * field_ref[tile] + coefficients_ref[3] * newest
 
-    hopping(place_ref, spatial_ref, field_ref, near_ref, across_ref, 0, emit)
+    hopping(
+        half,
+        lambda owner, c, rows: spatial_ref[owner, 0, c, rows, :],
+        lambda tile: field_ref[tile],
+        lambda tile: jnp.where(first, near(tile), far(tile)),
+        lambda tile: jnp.where(first, far(tile), near(tile)),
+        emit,
+    )
     for c in range(6):
         for block in range(2):
             mine, theirs = work[c * 4 + block], work[c * 4 + 2 + block]
@@ -462,19 +644,18 @@
                     out_ref[pl.ds(block * 96 + c * 4 + h * 2 + side, 4, stride=24), :] = value[4 * side : 4 * side + 4, :]
 
 
-def call(kernel, shapes, inputs, scratch=(), scalars=1):
+def call(kernel, shapes, inputs, scratch=(), scalars=1, space=pltpu.VMEM):
     smem = pl.BlockSpec(memory_space=pltpu.SMEM)
     vmem = pl.BlockSpec(memory_space=pltpu.VMEM)
     outs = [jax.ShapeDtypeStruct(shape, F32) for shape in shapes]
-    result = pl.pallas_call(
+    return pl.pallas_call(
         kernel,
         out_shape=outs,
-        in_specs=[smem] * scalars + [vmem] * (len(inputs) - scalars),
+        in_specs=[smem] * scalars + [pl.BlockSpec(memory_space=space)] * (len(inputs) - scalars),
         out_specs=[vmem] * len(outs),
-        scratch_shapes=[pltpu.VMEM(shape + TILE, F32) for shape in scratch],
+        scratch_shapes=[pltpu.VMEM(shape, F32) if isinstance(shape, tuple) else shape for shape in scratch],
         compiler_params=pltpu.CompilerParams(vmem_limit_bytes=8 << 20),
     )(*inputs)
-    return result
 
 
 def pairs(mesh):
@@ -500,51 +681,51 @@
     t = lax.axis_index(("grp", "ta"))
     x = lax.axis_index("xyz")
     place = jnp.stack([t % 2, x % 2, lax.axis_index("grp")]).astype(jnp.int32)
-    own, packed, fields = call(
+    raw = [links.reshape(144, 128), momenta.reshape(144, 128), vectors.reshape(192, 128)]
+    own, packed, send = call(
         split_kernel,
-        [(18,) + TILE, (8,) + TILE, (24,) + TILE],
-        [place, links.reshape(144, 128), momenta.reshape(144, 128), vectors.reshape(192, 128)],
-    )
-    forces = [(3, 18), (3, 18)]
-
-    def exchange(values, extra=None):
-        count = values.shape[0]
-        near = meet(values, chip)
-        sides = meet(meet(near, time), chip)
-        inputs = [place, values, sides] + ([] if extra is None else [extra])
-        more = 0 if extra is None else extra.shape[0]
-        (sent,) = call(
-            functools.partial(bundle_kernel, count, more), [(count + count // 2 + more,) + TILE], inputs
-        )
-        return near, sides, meet(sent, across)
-
-    near, sides, far = exchange(own, fields)
-    fields_near, fields_far = meet(fields, chip), far
-    halo, packed = call(
-        first_kernel, [(4, 18) + TILE, (8,) + TILE], [place, own, packed, near, sides, far], forces
-    )
+        [(18,) + TILE, (8,) + TILE, (36,) + TILE],
+        [place] + raw,
+        [value.shape for value in raw] + [pltpu.SemaphoreType.DMA((3,))],
+        space=pltpu.HBM,
+    )
+    forces = [(3, 18) + TILE, (3, 18) + TILE]
+
+    near = meet(send, chip)
+    sides = meet(meet(near[:, :12], time), chip)
+    (bundle,) = call(first_bundle_kernel, [(104,) + TILE], [place, send, packed, near, sides])
+    far = meet(bundle, across)
+    halo, pushed, far_packed = call(
+        first_kernel,
+        [(4, 18) + TILE, (12,) + TILE, (8,) + TILE],
+        [place, own, packed, near, sides, far],
+        forces + [(18,) + TILE, (4, 18) + TILE],
+    )
+    fields, fields_near, fields_far = send, near, far
+
+    near = meet(pushed, chip)
+    sides = meet(meet(near, time), chip)
     own, halo, packed = call(
         middle_kernel,
         [(18,) + TILE, (4, 18) + TILE, (8,) + TILE],
-        [place, own, halo, packed, *exchange(packed)],
+        [place, own, halo, pushed, far_packed, near, sides],
         forces,
     )
+
+    near = meet(packed, chip)
+    sides = meet(meet(near, time), chip)
+    (bundle,) = call(last_bundle_kernel, [(21,) + TILE], [place, own, halo, packed, near, sides])
     own, halo, spatial = call(
         last_drift_kernel,
-        [(18,) + TILE, (4, 18) + TILE, (18,) + TILE],
-        [place, own, halo, packed, *exchange(packed)],
-    )
+        [(18,) + TILE, (4, 18) + TILE, (2, 18) + TILE],
+        [place, own, halo, packed, near, sides, meet(bundle, across)],
+    )
+
     spatial = meet(spatial, halves)
-    (one,) = call(
-        functools.partial(first_hop_kernel, 27),
-        [(24,) + TILE],
-        [place, spatial, fields, fields_near, fields_far],
-    )
-    (two,) = call(
-        next_hop_kernel,
-        [(24,) + TILE],
-        [place, spatial, one, fields, meet(one, chip), meet(one, across)],
-    )
+    one, far_one = call(
+        first_hop_kernel, [(24,) + TILE, (24,) + TILE], [place, spatial, fields, fields_near, fields_far]
+    )
+    (two,) = call(second_hop_kernel, [(24,) + TILE], [place, spatial, one, fields, meet(one, chip), far_one])
     new_links, new_momenta = call(
         last_force_kernel, [(144, 128), (144, 128)], [own, halo, packed], forces, scalars=0
     )
@@ -552,7 +733,7 @@
         last_hop_kernel,
         [(192, 128)],
         [place, coefficients, spatial, two, one, fields, meet(two, chip), meet(two, across)],
-        [(24,)],
+        [(24,) + TILE],
         scalars=2,
     )
     return (

time: 114 us -> 101 us (0.89)
  blocking collectives: 99.8 us -> 85.4 us
    all_gather x18 -> x15, blocking collectives: 99.8 us -> 85.4 us  [meet(): return lax.all_gather(values, AXES, axis_index_groups=which)]
    pallas_call x11 -> x10, Pallas kernels: 10.2 us -> 11 us  [call(): pl.pallas_call(kernel, out_shape=outs, in_specs=[smem] * scalars + [pl.Bl...]
where the time goes in v2:
time: 101 us; the launch traced here: 100 us
  blocking collectives  85.4 us (85%)
  Pallas kernels  11 us (11%)
  local copies, waits for them, and re-layouts  3.22 us (3%)
    all_gather x15, blocking collectives, meet(): return lax.all_gather(values, AXES, axis_index_groups=which)  85.4 us
    pallas_call x10, Pallas kernels, call(): pl.pallas_call(kernel, out_shape=outs, in_specs=[smem] * scalars + [pl.Bl...  11 us
    unnamed x8, local copies, waits for them, and re-layouts  3.21 us

profile of v2, /device:TPU:112, one launch (start us, length us, event | category | flops | bytes accessed | tf_op | source)
XLA Modules:
  0.0 100.5 jit_solution(8653740162207733866)
XLA Ops:
  1.5 0.9 copy-done
  2.4 0.9 copy-done.2
  3.3 1.0 shard_map.67
  4.3 2.0 %all-gather = f32[72,8,128]{2,1,0:T(8,128)S(1)} all-gather(f32[36,8,128]{2,1,0:T(8,128)S(1)} %get-tuple-element.21.send_ref.field_ref.older_ref.oldest_ref), channel_id=2, replica_groups={{0,1},{2,3},{4,5},{6,7},{8,9},{10,11},{12,13},{14,15},{16,17},{18,19},{..., dimensions={0}, use_global_device_ids=true | all-gather | bytes 442368 | tf_op jit(solution)/shard_map/all_gather | solution.py:679
  6.3 5.3 %all-gather.1 = f32[4,12,8,128]{3,2,1,0:T(8,128)S(1)} all-gather(f32[2,12,8,128]{3,2,1,0:T(8,128)S(1)} %slice.4), channel_id=3, replica_groups={{0,64},{128,192},{256,320},{384,448},{512,576},{640,704},{768,832},{896..., dimensions={0}, use_global_device_ids=true | all-gather | bytes 294912 | tf_op jit(solution)/shard_map/all_gather | solution.py:679
  11.6 2.8 %all-gather.2 = f32[4,2,12,8,128]{4,3,2,1,0:T(8,128)S(1)} all-gather(f32[2,2,12,8,128]{4,3,2,1,0:T(8,128)S(1)} %bitcast.50), channel_id=4, replica_groups={{0,1},{2,3},{4,5},{6,7},{8,9},{10,11},{12,13},{14,15},{16,17},{18,19},{..., dimensions={0}, use_global_device_ids=true | all-gather | bytes 589824 | tf_op jit(solution)/shard_map/all_gather | solution.py:679
  14.9 27.1 %all-gather.3 = f32[208,8,128]{2,1,0:T(8,128)S(1)} all-gather(f32[104,8,128]{2,1,0:T(8,128)S(1)} %shard_map.68), channel_id=5, replica_groups={{1,2},{3,4},{5,6},{7,8},{9,10},{11,12},{13,14},{15,16},{17,18},{19,20},..., dimensions={0}, use_global_device_ids=true | all-gather | bytes 1277952 | tf_op jit(solution)/shard_map/all_gather | solution.py:679
  42.1 1.8 %shard_map.69 = (f32[4,18,8,128]{3,2,1,0:T(8,128)S(1)}, f32[12,8,128]{2,1,0:T(8,128)S(1)}, f32[8,8,128]{2,1,0:T(8,128)S(1)}) custom-call(s32[3]{0:T(128)S(1)} %pad_add_fusion.place_ref, f32[18,8,128]{2,1,0:T(8,128)S(1)} %get-tuple-element.19.own_ref, f32[8,8,128]{2,1,0:T(8,128)S(1)} %get-tuple-element.20.packed_ref, f32[2,36,8,128]{3,2,1,0:T(8,128)S(1)} %bitcast.28, ...), custom_call_target="tpu_custom_call" | custom-call | tf_op jit(solution)/shard_map/pallas_call | solution.py:651
  43.9 1.9 %all-gather.4 = f32[24,8,128]{2,1,0:T(8,128)S(1)} all-gather(f32[12,8,128]{2,1,0:T(8,128)S(1)} %get-tuple-element.23.send_ref), channel_id=6, replica_groups={{0,1},{2,3},{4,5},{6,7},{8,9},{10,11},{12,13},{14,15},{16,17},{18,19},{..., dimensions={0}, use_global_device_ids=true | all-gather | bytes 147456 | tf_op jit(solution)/shard_map/all_gather | solution.py:679
  45.7 5.3 %all-gather.5 = f32[4,12,8,128]{3,2,1,0:T(8,128)S(1)} all-gather(f32[2,12,8,128]{3,2,1,0:T(8,128)S(1)} %bitcast.41), channel_id=7, replica_groups={{0,64},{128,192},{256,320},{384,448},{512,576},{640,704},{768,832},{896..., dimensions={0}, use_global_device_ids=true | all-gather | bytes 294912 | tf_op jit(solution)/shard_map/all_gather | solution.py:679
  51.0 2.8 %all-gather.6 = f32[4,2,12,8,128]{4,3,2,1,0:T(8,128)S(1)} all-gather(f32[2,2,12,8,128]{4,3,2,1,0:T(8,128)S(1)} %bitcast.51), channel_id=8, replica_groups={{0,1},{2,3},{4,5},{6,7},{8,9},{10,11},{12,13},{14,15},{16,17},{18,19},{..., dimensions={0}, use_global_device_ids=true | all-gather | bytes 589824 | tf_op jit(solution)/shard_map/all_gather | solution.py:679
  53.8 1.4 %shard_map.70 = (f32[18,8,128]{2,1,0:T(8,128)S(1)}, f32[4,18,8,128]{3,2,1,0:T(8,128)S(1)}, f32[8,8,128]{2,1,0:T(8,128)S(1)}) custom-call(s32[3]{0:T(128)S(1)} %pad_add_fusion.place_ref, f32[18,8,128]{2,1,0:T(8,128)S(1)} %get-tuple-element.19.own_ref, f32[4,18,8,128]{3,2,1,0:T(8,128)S(1)} %get-tuple-element.22.halo_ref, ...), custom_call_target="tpu_custom_call" | custom-call | tf_op jit(solution)/shard_map/pallas_call | solution.py:651
  55.2 1.9 %all-gather.7 = f32[16,8,128]{2,1,0:T(8,128)S(1)} all-gather(f32[8,8,128]{2,1,0:T(8,128)S(1)} %get-tuple-element.27.packed_ref), channel_id=9, replica_groups={{0,1},{2,3},{4,5},{6,7},{8,9},{10,11},{12,13},{14,15},{16,17},{18,19},{..., dimensions={0}, use_global_device_ids=true | all-gather | bytes 98304 | tf_op jit(solution)/shard_map/all_gather | solution.py:679
  57.1 4.9 %all-gather.8 = f32[4,8,8,128]{3,2,1,0:T(8,128)S(1)} all-gather(f32[2,8,8,128]{3,2,1,0:T(8,128)S(1)} %bitcast.38), channel_id=10, replica_groups={{0,64},{128,192},{256,320},{384,448},{512,576},{640,704},{768,832},{896..., dimensions={0}, use_global_device_ids=true | all-gather | bytes 196608 | tf_op jit(solution)/shard_map/all_gather | solution.py:679
  62.0 2.9 %all-gather.9 = f32[4,2,8,8,128]{4,3,2,1,0:T(8,128)S(1)} all-gather(f32[2,2,8,8,128]{4,3,2,1,0:T(8,128)S(1)} %bitcast.52), channel_id=11, replica_groups={{0,1},{2,3},{4,5},{6,7},{8,9},{10,11},{12,13},{14,15},{16,17},{18,19},{..., dimensions={0}, use_global_device_ids=true | all-gather | bytes 393216 | tf_op jit(solution)/shard_map/all_gather | solution.py:679
  65.6 8.8 %all-gather.10 = f32[42,8,128]{2,1,0:T(8,128)S(1)} all-gather(f32[21,8,128]{2,1,0:T(8,128)S(1)} %shard_map.71), channel_id=12, replica_groups={{1,2},{3,4},{5,6},{7,8},{9,10},{11,12},{13,14},{15,16},{17,18},{19,20},..., dimensions={0}, use_global_device_ids=true | all-gather | bytes 258048 | tf_op jit(solution)/shard_map/all_gather | solution.py:679
  75.2 1.3 %shard_map.73 = (f32[144,128]{1,0:T(8,128)}, f32[144,128]{1,0:T(8,128)}) custom-call(f32[18,8,128]{2,1,0:T(8,128)S(1)} %get-tuple-element.28.own_ref, f32[4,18,8,128]{3,2,1,0:T(8,128)S(1)} %get-tuple-element.29.halo_ref, f32[8,8,128]{2,1,0:T(8,128)S(1)} %get-tuple-element.27.packed_ref), custom_call_target="tpu_custom_call" | custom-call | tf_op jit(solution)/shard_map/pallas_call | solution.py:651
  76.5 6.3 %all-gather.11 = f32[4,18,8,128]{3,2,1,0:T(8,128)S(1)} all-gather(f32[2,18,8,128]{3,2,1,0:T(8,128)S(1)} %get-tuple-element.32), channel_id=13, replica_groups={{0,512},{1,513},{2,514},{3,515},{4,516},{5,517},{6,518},{7,519},{8,520}..., dimensions={0}, use_global_device_ids=true | all-gather | bytes 442368 | tf_op jit(solution)/shard_map/all_gather | solution.py:679
  82.8 1.2 %shard_map.74 = (f32[24,8,128]{2,1,0:T(8,128)S(1)}, f32[24,8,128]{2,1,0:T(8,128)S(1)}) custom-call(s32[3]{0:T(128)S(1)} %pad_add_fusion.place_ref, f32[2,2,18,8,128]{4,3,2,1,0:T(8,128)S(1)} %bitcast.30, f32[36,8,128]{2,1,0:T(8,128)S(1)} %get-tuple-element.21.send_ref.field_ref.older_ref.oldest_ref, f32[2,36,8,128]{3,2,1,0:T(8,128)S(1)} %bitcast.29, ...), custom_call_target="tpu_custom_call" | custom-call | tf_op jit(solution)/shard_map/pallas_call | solution.py:651
  84.0 1.9 %all-gather.12 = f32[48,8,128]{2,1,0:T(8,128)S(1)} all-gather(f32[24,8,128]{2,1,0:T(8,128)S(1)} %get-tuple-element.33.field_ref.older_ref), channel_id=14, replica_groups={{0,1},{2,3},{4,5},{6,7},{8,9},{10,11},{12,13},{14,15},{16,17},{18,19},{..., dimensions={0}, use_global_device_ids=true | all-gather | bytes 294912 | tf_op jit(solution)/shard_map/all_gather | solution.py:679
  85.9 0.9 shard_map.75.field_ref
  86.8 1.9 %all-gather.13 = f32[48,8,128]{2,1,0:T(8,128)S(1)} all-gather(f32[24,8,128]{2,1,0:T(8,128)S(1)} %shard_map.75.field_ref), channel_id=15, replica_groups={{0,1},{2,3},{4,5},{6,7},{8,9},{10,11},{12,13},{14,15},{16,17},{18,19},{..., dimensions={0}, use_global_device_ids=true | all-gather | bytes 294912 | tf_op jit(solution)/shard_map/all_gather | solution.py:679
  88.7 9.5 %all-gather.14 = f32[48,8,128]{2,1,0:T(8,128)S(1)} all-gather(f32[24,8,128]{2,1,0:T(8,128)S(1)} %shard_map.75.field_ref), channel_id=16, replica_groups={{1,2},{3,4},{5,6},{7,8},{9,10},{11,12},{13,14},{15,16},{17,18},{19,20},..., dimensions={0}, use_global_device_ids=true | all-gather | bytes 294912 | tf_op jit(solution)/shard_map/all_gather | solution.py:679
  98.9 1.5 %shard_map.76 = f32[192,128]{1,0:T(8,128)} custom-call(s32[3]{0:T(128)S(1)} %pad_add_fusion.place_ref, f32[4]{0:T(128)S(1)} %copy-done.3, f32[2,2,18,8,128]{4,3,2,1,0:T(8,128)S(1)} %bitcast.32, f32[24,8,128]{2,1,0:T(8,128)S(1)} %shard_map.75.field_ref, f32[24,8,128]{2,1,0:T(8,128)S(1)} %get-tuple-element.33.field_ref.older_ref, ...), custom_call_target="tpu_custom_call" | custom-call | tf_op jit(solution)/shard_map/pallas_call | solution.py:651
  (11 shorter events, 3.5 us)
Async XLA Ops:
  0.6 0.9 copy-start.1
  1.5 0.9 copy-start
  2.4 0.9 copy-start.2
  98.3 0.7 copy-start.3

commit v3 on v2

--- a/solution.py
+++ b/solution.py
@@ -611,8 +611,11 @@
 
 
 def last_hop_kernel(
-    place_ref, coefficients_ref, spatial_ref, field_ref, older_ref, oldest_ref, near_ref, across_ref, out_ref, work
+    place_ref, coefficients_hbm, spatial_ref, field_ref, older_ref, oldest_ref, near_ref, across_ref,
+    out_ref, work, coefficients_ref, sem,
 ):
+    copy = pltpu.make_async_copy(coefficients_hbm, coefficients_ref, sem)
+    copy.start()
     odd_space, half = place_ref[1], place_ref[2]
     first = odd_space == 0
 
@@ -623,9 +626,7 @@
         return across_ref[odd_space, tile]
 
     def emit(tile, value):
-        newest = 2.0 * value - older_ref[tile]
-        total = coefficients_ref[0] * oldest_ref[12 + tile] + coefficients_ref[1] * older_ref[tile]
-        work[tile] = total + coefficients_ref[2] * field_ref[tile] + coefficients_ref[3] * newest
+        work[tile] = 2.0 * value - older_ref[tile]
 
     hopping(
         half,
@@ -635,24 +636,36 @@
         lambda tile: jnp.where(first, far(tile), near(tile)),
         emit,
     )
+    copy.wait()
+
+    def total(tile):
+        value = coefficients_ref[0] * oldest_ref[12 + tile] + coefficients_ref[1] * older_ref[tile]
+        return value + coefficients_ref[2] * field_ref[tile] + coefficients_ref[3] * work[tile]
+
     for c in range(6):
         for block in range(2):
-            mine, theirs = work[c * 4 + block], work[c * 4 + 2 + block]
+            mine, theirs = total(c * 4 + block), total(c * 4 + 2 + block)
             for h in range(2):
                 value = jnp.where(half == h, mine, theirs)
                 for side in range(2):
                     out_ref[pl.ds(block * 96 + c * 4 + h * 2 + side, 4, stride=24), :] = value[4 * side : 4 * side + 4, :]
 
 
-def call(kernel, shapes, inputs, scratch=(), scalars=1, space=pltpu.VMEM):
-    smem = pl.BlockSpec(memory_space=pltpu.SMEM)
-    vmem = pl.BlockSpec(memory_space=pltpu.VMEM)
-    outs = [jax.ShapeDtypeStruct(shape, F32) for shape in shapes]
+def call(kernel, shapes, inputs, scratch=(), scalars=1, hbm=()):
+    def spec(position):
+        if position < scalars:
+            return pl.BlockSpec(memory_space=pltpu.SMEM)
+        return pl.BlockSpec(memory_space=pltpu.HBM if position in hbm else pltpu.VMEM)
+
+    inputs = [
+        pltpu.with_memory_space_constraint(value, pltpu.HBM) if position in hbm else value
+        for position, value in enumerate(inputs)
+    ]
     return pl.pallas_call(
         kernel,
-        out_shape=outs,
-        in_specs=[smem] * scalars + [pl.BlockSpec(memory_space=space)] * (len(inputs) - scalars),
-        out_specs=[vmem] * len(outs),
+        out_shape=[jax.ShapeDtypeStruct(shape, F32) for shape in shapes],
+        in_specs=[spec(position) for position in range(len(inputs))],
+        out_specs=[pl.BlockSpec(memory_space=pltpu.VMEM)] * len(shapes),
         scratch_shapes=[pltpu.VMEM(shape, F32) if isinstance(shape, tuple) else shape for shape in scratch],
         compiler_params=pltpu.CompilerParams(vmem_limit_bytes=8 << 20),
     )(*inputs)
@@ -687,7 +700,7 @@
         [(18,) + TILE, (8,) + TILE, (36,) + TILE],
         [place] + raw,
         [value.shape for value in raw] + [pltpu.SemaphoreType.DMA((3,))],
-        space=pltpu.HBM,
+        hbm=(1, 2, 3),
     )
     forces = [(3, 18) + TILE, (3, 18) + TILE]
 
@@ -733,8 +746,8 @@
         last_hop_kernel,
         [(192, 128)],
         [place, coefficients, spatial, two, one, fields, meet(two, chip), meet(two, across)],
-        [(24,) + TILE],
-        scalars=2,
+        [(24,) + TILE, pltpu.SMEM((4,), F32), pltpu.SemaphoreType.DMA],
+        hbm=(1,),
     )
     return (
         new_links.reshape(links.shape),

time: 101 us -> 98.7 us (0.977)
  local copies, waits for them, and re-layouts: 3.22 us -> 0.01 us
  Pallas kernels: 11 us -> 12.2 us
    unnamed x8 -> x0, local copies, waits for them, and re-layouts: 3.21 us -> none
    pallas_call x10, Pallas kernels: 11 us -> 12.2 us  [call(): pl.pallas_call(kernel, out_shape=[jax.ShapeDtypeStruct(shape, F32) for sh...]
where the time goes in v3:
time: 98.7 us; the launch traced here: 98.4 us
  blocking collectives  85.4 us (87%)
  Pallas kernels  12.2 us (12%)
    all_gather x15, blocking collectives, meet(): return lax.all_gather(values, AXES, axis_index_groups=which)  85.4 us
    pallas_call x10, Pallas kernels, call(): pl.pallas_call(kernel, out_shape=[jax.ShapeDtypeStruct(shape, F32) for sh...  12.2 us

profile of v3, /device:TPU:112, one launch (start us, length us, event | category | flops | bytes accessed | tf_op | source)
XLA Modules:
  0.0 98.4 jit_solution(4252067947698588403)
XLA Ops:
  0.7 1.5 %shard_map.67 = (f32[18,8,128]{2,1,0:T(8,128)S(1)}, f32[8,8,128]{2,1,0:T(8,128)S(1)}, f32[36,8,128]{2,1,0:T(8,128)S(1)}) custom-call(s32[3]{0:T(128)S(1)} %pad_add_fusion.place_ref, f32[144,128]{1,0:T(8,128)} %bitcast.52, f32[144,128]{1,0:T(8,128)} %bitcast.53, f32[192,128]{1,0:T(8,128)} %bitcast.51), custom_call_target="tpu_custom_call" | custom-call | tf_op jit(solution)/shard_map/pallas_call | solution.py:664
  2.3 2.0 %all-gather = f32[72,8,128]{2,1,0:T(8,128)S(1)} all-gather(f32[36,8,128]{2,1,0:T(8,128)S(1)} %get-tuple-element.21.send_ref.field_ref.older_ref.oldest_ref), channel_id=2, replica_groups={{0,1},{2,3},{4,5},{6,7},{8,9},{10,11},{12,13},{14,15},{16,17},{18,19},{..., dimensions={0}, use_global_device_ids=true | all-gather | bytes 442368 | tf_op jit(solution)/shard_map/all_gather | solution.py:692
  4.3 5.3 %all-gather.1 = f32[4,12,8,128]{3,2,1,0:T(8,128)S(1)} all-gather(f32[2,12,8,128]{3,2,1,0:T(8,128)S(1)} %slice.4), channel_id=3, replica_groups={{0,64},{128,192},{256,320},{384,448},{512,576},{640,704},{768,832},{896..., dimensions={0}, use_global_device_ids=true | all-gather | bytes 294912 | tf_op jit(solution)/shard_map/all_gather | solution.py:692
  9.6 2.8 %all-gather.2 = f32[4,2,12,8,128]{4,3,2,1,0:T(8,128)S(1)} all-gather(f32[2,2,12,8,128]{4,3,2,1,0:T(8,128)S(1)} %bitcast.47), channel_id=4, replica_groups={{0,1},{2,3},{4,5},{6,7},{8,9},{10,11},{12,13},{14,15},{16,17},{18,19},{..., dimensions={0}, use_global_device_ids=true | all-gather | bytes 589824 | tf_op jit(solution)/shard_map/all_gather | solution.py:692
  13.0 27.1 %all-gather.3 = f32[208,8,128]{2,1,0:T(8,128)S(1)} all-gather(f32[104,8,128]{2,1,0:T(8,128)S(1)} %shard_map.68), channel_id=5, replica_groups={{1,2},{3,4},{5,6},{7,8},{9,10},{11,12},{13,14},{15,16},{17,18},{19,20},..., dimensions={0}, use_global_device_ids=true | all-gather | bytes 1277952 | tf_op jit(solution)/shard_map/all_gather | solution.py:692
  40.1 1.8 %shard_map.69 = (f32[4,18,8,128]{3,2,1,0:T(8,128)S(1)}, f32[12,8,128]{2,1,0:T(8,128)S(1)}, f32[8,8,128]{2,1,0:T(8,128)S(1)}) custom-call(s32[3]{0:T(128)S(1)} %pad_add_fusion.place_ref, f32[18,8,128]{2,1,0:T(8,128)S(1)} %get-tuple-element.19.own_ref, f32[8,8,128]{2,1,0:T(8,128)S(1)} %get-tuple-element.20.packed_ref, f32[2,36,8,128]{3,2,1,0:T(8,128)S(1)} %bitcast.28, ...), custom_call_target="tpu_custom_call" | custom-call | tf_op jit(solution)/shard_map/pallas_call | solution.py:664
  41.9 1.9 %all-gather.4 = f32[24,8,128]{2,1,0:T(8,128)S(1)} all-gather(f32[12,8,128]{2,1,0:T(8,128)S(1)} %get-tuple-element.23.send_ref), channel_id=6, replica_groups={{0,1},{2,3},{4,5},{6,7},{8,9},{10,11},{12,13},{14,15},{16,17},{18,19},{..., dimensions={0}, use_global_device_ids=true | all-gather | bytes 147456 | tf_op jit(solution)/shard_map/all_gather | solution.py:692
  43.8 5.3 %all-gather.5 = f32[4,12,8,128]{3,2,1,0:T(8,128)S(1)} all-gather(f32[2,12,8,128]{3,2,1,0:T(8,128)S(1)} %bitcast.41), channel_id=7, replica_groups={{0,64},{128,192},{256,320},{384,448},{512,576},{640,704},{768,832},{896..., dimensions={0}, use_global_device_ids=true | all-gather | bytes 294912 | tf_op jit(solution)/shard_map/all_gather | solution.py:692
  49.0 2.8 %all-gather.6 = f32[4,2,12,8,128]{4,3,2,1,0:T(8,128)S(1)} all-gather(f32[2,2,12,8,128]{4,3,2,1,0:T(8,128)S(1)} %bitcast.48), channel_id=8, replica_groups={{0,1},{2,3},{4,5},{6,7},{8,9},{10,11},{12,13},{14,15},{16,17},{18,19},{..., dimensions={0}, use_global_device_ids=true | all-gather | bytes 589824 | tf_op jit(solution)/shard_map/all_gather | solution.py:692
  51.9 1.4 %shard_map.70 = (f32[18,8,128]{2,1,0:T(8,128)S(1)}, f32[4,18,8,128]{3,2,1,0:T(8,128)S(1)}, f32[8,8,128]{2,1,0:T(8,128)S(1)}) custom-call(s32[3]{0:T(128)S(1)} %pad_add_fusion.place_ref, f32[18,8,128]{2,1,0:T(8,128)S(1)} %get-tuple-element.19.own_ref, f32[4,18,8,128]{3,2,1,0:T(8,128)S(1)} %get-tuple-element.22.halo_ref, ...), custom_call_target="tpu_custom_call" | custom-call | tf_op jit(solution)/shard_map/pallas_call | solution.py:664
  53.3 1.9 %all-gather.7 = f32[16,8,128]{2,1,0:T(8,128)S(1)} all-gather(f32[8,8,128]{2,1,0:T(8,128)S(1)} %get-tuple-element.27.packed_ref), channel_id=9, replica_groups={{0,1},{2,3},{4,5},{6,7},{8,9},{10,11},{12,13},{14,15},{16,17},{18,19},{..., dimensions={0}, use_global_device_ids=true | all-gather | bytes 98304 | tf_op jit(solution)/shard_map/all_gather | solution.py:692
  55.1 4.9 %all-gather.8 = f32[4,8,8,128]{3,2,1,0:T(8,128)S(1)} all-gather(f32[2,8,8,128]{3,2,1,0:T(8,128)S(1)} %bitcast.38), channel_id=10, replica_groups={{0,64},{128,192},{256,320},{384,448},{512,576},{640,704},{768,832},{896..., dimensions={0}, use_global_device_ids=true | all-gather | bytes 196608 | tf_op jit(solution)/shard_map/all_gather | solution.py:692
  60.1 2.9 %all-gather.9 = f32[4,2,8,8,128]{4,3,2,1,0:T(8,128)S(1)} all-gather(f32[2,2,8,8,128]{4,3,2,1,0:T(8,128)S(1)} %bitcast.49), channel_id=11, replica_groups={{0,1},{2,3},{4,5},{6,7},{8,9},{10,11},{12,13},{14,15},{16,17},{18,19},{..., dimensions={0}, use_global_device_ids=true | all-gather | bytes 393216 | tf_op jit(solution)/shard_map/all_gather | solution.py:692
  63.0 0.6 shard_map.71
  63.6 8.8 %all-gather.10 = f32[42,8,128]{2,1,0:T(8,128)S(1)} all-gather(f32[21,8,128]{2,1,0:T(8,128)S(1)} %shard_map.71), channel_id=12, replica_groups={{1,2},{3,4},{5,6},{7,8},{9,10},{11,12},{13,14},{15,16},{17,18},{19,20},..., dimensions={0}, use_global_device_ids=true | all-gather | bytes 258048 | tf_op jit(solution)/shard_map/all_gather | solution.py:692
  72.4 0.8 shard_map.72
  73.2 1.3 %shard_map.73 = (f32[144,128]{1,0:T(8,128)}, f32[144,128]{1,0:T(8,128)}) custom-call(f32[18,8,128]{2,1,0:T(8,128)S(1)} %get-tuple-element.28.own_ref, f32[4,18,8,128]{3,2,1,0:T(8,128)S(1)} %get-tuple-element.29.halo_ref, f32[8,8,128]{2,1,0:T(8,128)S(1)} %get-tuple-element.27.packed_ref), custom_call_target="tpu_custom_call" | custom-call | tf_op jit(solution)/shard_map/pallas_call | solution.py:664
  74.5 6.3 %all-gather.11 = f32[4,18,8,128]{3,2,1,0:T(8,128)S(1)} all-gather(f32[2,18,8,128]{3,2,1,0:T(8,128)S(1)} %get-tuple-element.32), channel_id=13, replica_groups={{0,512},{1,513},{2,514},{3,515},{4,516},{5,517},{6,518},{7,519},{8,520}..., dimensions={0}, use_global_device_ids=true | all-gather | bytes 442368 | tf_op jit(solution)/shard_map/all_gather | solution.py:692
  80.8 1.2 %shard_map.74 = (f32[24,8,128]{2,1,0:T(8,128)S(1)}, f32[24,8,128]{2,1,0:T(8,128)S(1)}) custom-call(s32[3]{0:T(128)S(1)} %pad_add_fusion.place_ref, f32[2,2,18,8,128]{4,3,2,1,0:T(8,128)S(1)} %bitcast.30, f32[36,8,128]{2,1,0:T(8,128)S(1)} %get-tuple-element.21.send_ref.field_ref.older_ref.oldest_ref, f32[2,36,8,128]{3,2,1,0:T(8,128)S(1)} %bitcast.29, ...), custom_call_target="tpu_custom_call" | custom-call | tf_op jit(solution)/shard_map/pallas_call | solution.py:664
  82.0 1.9 %all-gather.12 = f32[48,8,128]{2,1,0:T(8,128)S(1)} all-gather(f32[24,8,128]{2,1,0:T(8,128)S(1)} %get-tuple-element.33.field_ref.older_ref), channel_id=14, replica_groups={{0,1},{2,3},{4,5},{6,7},{8,9},{10,11},{12,13},{14,15},{16,17},{18,19},{..., dimensions={0}, use_global_device_ids=true | all-gather | bytes 294912 | tf_op jit(solution)/shard_map/all_gather | solution.py:692
  83.9 0.9 shard_map.75.field_ref
  84.8 1.9 %all-gather.13 = f32[48,8,128]{2,1,0:T(8,128)S(1)} all-gather(f32[24,8,128]{2,1,0:T(8,128)S(1)} %shard_map.75.field_ref), channel_id=15, replica_groups={{0,1},{2,3},{4,5},{6,7},{8,9},{10,11},{12,13},{14,15},{16,17},{18,19},{..., dimensions={0}, use_global_device_ids=true | all-gather | bytes 294912 | tf_op jit(solution)/shard_map/all_gather | solution.py:692
  86.8 9.5 %all-gather.14 = f32[48,8,128]{2,1,0:T(8,128)S(1)} all-gather(f32[24,8,128]{2,1,0:T(8,128)S(1)} %shard_map.75.field_ref), channel_id=16, replica_groups={{1,2},{3,4},{5,6},{7,8},{9,10},{11,12},{13,14},{15,16},{17,18},{19,20},..., dimensions={0}, use_global_device_ids=true | all-gather | bytes 294912 | tf_op jit(solution)/shard_map/all_gather | solution.py:692
  96.3 2.1 %shard_map.76 = f32[192,128]{1,0:T(8,128)} custom-call(s32[3]{0:T(128)S(1)} %pad_add_fusion.place_ref, f32[4]{0:T(128)} %coefficients_hbm.1, f32[2,2,18,8,128]{4,3,2,1,0:T(8,128)S(1)} %bitcast.32, f32[24,8,128]{2,1,0:T(8,128)S(1)} %shard_map.75.field_ref, f32[24,8,128]{2,1,0:T(8,128)S(1)} %get-tuple-element.33.field_ref.older_ref, ...), custom_call_target="tpu_custom_call" | custom-call | tf_op jit(solution)/shard_map/pallas_call | solution.py:664
  (3 shorter events, 0.7 us)

commit v4 on v3

--- a/solution.py
+++ b/solution.py
@@ -496,14 +496,13 @@
             momenta_ref[d * 36 + 2 * c : d * 36 + 2 * c + 2, :] = full[c][2 * d : 2 * d + 2, :]
 
 
-def hopping(half, links, field, ahead, behind, emit):
+def hopping(sides, links, field, ahead, behind, emit):
     row, lane = iotas()
-    for side in range(2):
-        owner = half if side == 0 else 1 - half
+    for side in sides:
 
         def link(d, c):
-            low = jnp.broadcast_to(links(owner, c, slice(2 * d, 2 * d + 1)), TILE)
-            high = jnp.broadcast_to(links(owner, c, slice(2 * d + 1, 2 * d + 2)), TILE)
+            low = jnp.broadcast_to(links(side, c, slice(2 * d, 2 * d + 1)), TILE)
+            high = jnp.broadcast_to(links(side, c, slice(2 * d + 1, 2 * d + 2)), TILE)
             return jnp.where(row < 4, low, high)
 
         totals = {}
@@ -550,9 +549,16 @@
                 emit(c * 4 + side * 2 + block, totals[block, c] * (-1.0 / 6.0))
 
 
-def first_hop_kernel(place_ref, spatial_ref, field_ref, near_ref, across_ref, out_ref, far_out_ref):
-    odd_space, half = place_ref[1], place_ref[2]
+def first_hop_kernel(side, place_ref, spatial_ref, field_ref, near_ref, across_ref, *rest):
+    odd_space = place_ref[1]
     first = odd_space == 0
+    out_ref, far_out_ref = rest[-2:]
+    if side == 1:
+        for c in range(6):
+            for block in range(2):
+                tile = c * 4 + block
+                out_ref[tile] = rest[0][tile]
+                far_out_ref[tile] = rest[1][tile]
 
     def own(tile):
         return field_ref[12 + tile]
@@ -573,16 +579,16 @@
         return emit
 
     hopping(
-        half,
-        lambda owner, c, rows: spatial_ref[owner, 0, c, rows, :],
+        (side,),
+        lambda _, c, rows: spatial_ref[0, c, rows, :],
         own,
         lambda tile: jnp.where(first, near(tile), far(tile)),
         lambda tile: jnp.where(first, far(tile), near(tile)),
         put(out_ref),
     )
     hopping(
-        half,
-        lambda owner, c, rows: spatial_ref[owner, 1, c, rows, :],
+        (side,),
+        lambda _, c, rows: spatial_ref[1, c, rows, :],
         far,
         lambda tile: jnp.where(first, own(tile), farther(tile)),
         lambda tile: jnp.where(first, farther(tile), own(tile)),
@@ -590,8 +596,8 @@
     )
 
 
-def second_hop_kernel(place_ref, spatial_ref, field_ref, older_ref, near_ref, far_ref, out_ref):
-    odd_space, half = place_ref[1], place_ref[2]
+def second_hop_kernel(place_ref, spatial_ref, other_ref, field_ref, older_ref, near_ref, far_ref, out_ref):
+    odd_space = place_ref[1]
     first = odd_space == 0
 
     def near(tile):
@@ -601,8 +607,8 @@
         out_ref[tile] = 2.0 * value - older_ref[12 + tile]
 
     hopping(
-        half,
-        lambda owner, c, rows: spatial_ref[owner, 0, c, rows, :],
+        (0, 1),
+        lambda side, c, rows: (other_ref if side else spatial_ref)[0, c, rows, :],
         lambda tile: field_ref[tile],
         lambda tile: jnp.where(first, near(tile), far_ref[tile]),
         lambda tile: jnp.where(first, far_ref[tile], near(tile)),
@@ -611,7 +617,7 @@
 
 
 def last_hop_kernel(
-    place_ref, coefficients_hbm, spatial_ref, field_ref, older_ref, oldest_ref, near_ref, across_ref,
+    place_ref, coefficients_hbm, spatial_ref, other_ref, field_ref, older_ref, oldest_ref, near_ref, across_ref,
     out_ref, work, coefficients_ref, sem,
 ):
     copy = pltpu.make_async_copy(coefficients_hbm, coefficients_ref, sem)
@@ -629,8 +635,8 @@
         work[tile] = 2.0 * value - older_ref[tile]
 
     hopping(
-        half,
-        lambda owner, c, rows: spatial_ref[owner, 0, c, rows, :],
+        (0, 1),
+        lambda side, c, rows: (other_ref if side else spatial_ref)[0, c, rows, :],
         lambda tile: field_ref[tile],
         lambda tile: jnp.where(first, near(tile), far(tile)),
         lambda tile: jnp.where(first, far(tile), near(tile)),
@@ -668,12 +674,12 @@
         out_specs=[pl.BlockSpec(memory_space=pltpu.VMEM)] * len(shapes),
         scratch_shapes=[pltpu.VMEM(shape, F32) if isinstance(shape, tuple) else shape for shape in scratch],
         compiler_params=pltpu.CompilerParams(vmem_limit_bytes=8 << 20),
+        cost_estimate=pl.CostEstimate(flops=4_000_000, bytes_accessed=4_000_000, transcendentals=0),
     )(*inputs)
 
 
 def pairs(mesh):
     times, spaces = mesh.shape["grp"] * mesh.shape["ta"], mesh.shape["xyz"]
-    offset = mesh.shape["ta"]
 
     def at(t, x):
         return (t % times) * spaces + x % spaces
@@ -681,12 +687,11 @@
     chip = [[at(t, x), at(t, x + 1)] for t in range(times) for x in range(0, spaces, 2)]
     across = [[at(t, x), at(t, x + 1)] for t in range(times) for x in range(1, spaces, 2)]
     time = [[at(t, x), at(t + 1, x)] for x in range(spaces) for t in range(x % 2, times, 2)]
-    halves = [[at(t, x), at(t + offset, x)] for t in range(offset) for x in range(spaces)]
-    return chip, across, time, halves
+    return chip, across, time
 
 
 def body(groups, links, momenta, vectors, coefficients):
-    chip, across, time, halves = groups
+    chip, across, time = groups
 
     def meet(values, which):
         return lax.all_gather(values, AXES, axis_index_groups=which)
@@ -734,18 +739,24 @@
         [place, own, halo, packed, near, sides, meet(bundle, across)],
     )
 
-    spatial = meet(spatial, halves)
+    other = lax.ppermute(spatial, "grp", [(0, 1), (1, 0)])
+    vectors_here = [fields, fields_near, fields_far]
     one, far_one = call(
-        first_hop_kernel, [(24,) + TILE, (24,) + TILE], [place, spatial, fields, fields_near, fields_far]
-    )
-    (two,) = call(second_hop_kernel, [(24,) + TILE], [place, spatial, one, fields, meet(one, chip), far_one])
+        functools.partial(first_hop_kernel, 0), [(24,) + TILE] * 2, [place, spatial] + vectors_here
+    )
     new_links, new_momenta = call(
         last_force_kernel, [(144, 128), (144, 128)], [own, halo, packed], forces, scalars=0
+    )
+    one, far_one = call(
+        functools.partial(first_hop_kernel, 1), [(24,) + TILE] * 2, [place, other] + vectors_here + [one, far_one]
+    )
+    (two,) = call(
+        second_hop_kernel, [(24,) + TILE], [place, spatial, other, one, fields, meet(one, chip), far_one]
     )
     (filtered,) = call(
         last_hop_kernel,
         [(192, 128)],
-        [place, coefficients, spatial, two, one, fields, meet(two, chip), meet(two, across)],
+        [place, coefficients, spatial, other, two, one, fields, meet(two, chip), meet(two, across)],
         [(24,) + TILE, pltpu.SMEM((4,), F32), pltpu.SemaphoreType.DMA],
         hbm=(1,),
     )

time: 98.7 us -> 98.2 us (level)
  blocking collectives: 85.4 us -> 79.2 us
  starting transfers between devices: 0 us -> 4.44 us
    all_gather x15 -> x14, blocking collectives: 85.4 us -> 79.2 us  [meet(): return lax.all_gather(values, AXES, axis_index_groups=which)]
    ppermute x0 -> x1, starting transfers between devices: none -> 4.44 us  [body(): other = lax.ppermute(spatial, 'grp', [(0, 1), (1, 0)])]
    pallas_call x10 -> x11, Pallas kernels: 12.2 us -> 12.5 us  [call(): pl.pallas_call(kernel, out_shape=[jax.ShapeDtypeStruct(shape, F32) for sh...]
  transfers between devices with their start and end apart: 0 -> 1, of which waited for: 0 -> 1; matrix products, arithmetic and copies ran while one was open for 0% -> 0% of each run, Pallas kernels for 0% -> 2%
where the time goes in v4:
time: 98.2 us; the launch traced here: 97.9 us
  blocking collectives  79.2 us (81%)
  Pallas kernels  12.5 us (13%)
  starting transfers between devices  4.44 us (5%)
    all_gather x14, blocking collectives, meet(): return lax.all_gather(values, AXES, axis_index_groups=which)  79.2 us
    pallas_call x11, Pallas kernels, call(): pl.pallas_call(kernel, out_shape=[jax.ShapeDtypeStruct(shape, F32) for sh...  12.5 us
    ppermute x1, starting transfers between devices, body(): other = lax.ppermute(spatial, 'grp', [(0, 1), (1, 0)])  4.44 us
  transfers between devices with their start and end apart: 1, of which 1 were waited for; matrix products, arithmetic and copies ran while one was open for 0% of the time, Pallas kernels for 2%

profile of v4, /device:TPU:112, one launch (start us, length us, event | category | flops | bytes accessed | tf_op | source)
XLA Modules:
  0.0 97.9 jit_solution(3098585050103558974)
XLA Ops:
  0.7 1.5 %shard_map.67 = (f32[18,8,128]{2,1,0:T(8,128)S(1)}, f32[8,8,128]{2,1,0:T(8,128)S(1)}, f32[36,8,128]{2,1,0:T(8,128)S(1)}) custom-call(s32[3]{0:T(128)S(1)} %pad_add_fusion.place_ref, f32[144,128]{1,0:T(8,128)} %bitcast.50, f32[144,128]{1,0:T(8,128)} %bitcast.51, f32[192,128]{1,0:T(8,128)} %bitcast.49), custom_call_target="tpu_custom_call" | custom-call | flops 4000000 | bytes 4000000 | tf_op jit(solution)/shard_map/pallas_call | solution.py:670
  2.3 2.0 %all-gather = f32[72,8,128]{2,1,0:T(8,128)S(1)} all-gather(f32[36,8,128]{2,1,0:T(8,128)S(1)} %get-tuple-element.23.send_ref.field_ref.older_ref.oldest_ref), channel_id=2, replica_groups={{0,1},{2,3},{4,5},{6,7},{8,9},{10,11},{12,13},{14,15},{16,17},{18,19},{..., dimensions={0}, use_global_device_ids=true | all-gather | bytes 442368 | tf_op jit(solution)/shard_map/all_gather | solution.py:697
  4.3 5.3 %all-gather.1 = f32[4,12,8,128]{3,2,1,0:T(8,128)S(1)} all-gather(f32[2,12,8,128]{3,2,1,0:T(8,128)S(1)} %slice.4), channel_id=3, replica_groups={{0,64},{128,192},{256,320},{384,448},{512,576},{640,704},{768,832},{896..., dimensions={0}, use_global_device_ids=true | all-gather | bytes 294912 | tf_op jit(solution)/shard_map/all_gather | solution.py:697
  9.6 2.8 %all-gather.2 = f32[4,2,12,8,128]{4,3,2,1,0:T(8,128)S(1)} all-gather(f32[2,2,12,8,128]{4,3,2,1,0:T(8,128)S(1)} %bitcast.45), channel_id=4, replica_groups={{0,1},{2,3},{4,5},{6,7},{8,9},{10,11},{12,13},{14,15},{16,17},{18,19},{..., dimensions={0}, use_global_device_ids=true | all-gather | bytes 589824 | tf_op jit(solution)/shard_map/all_gather | solution.py:697
  13.0 27.1 %all-gather.3 = f32[208,8,128]{2,1,0:T(8,128)S(1)} all-gather(f32[104,8,128]{2,1,0:T(8,128)S(1)} %shard_map.68), channel_id=5, replica_groups={{1,2},{3,4},{5,6},{7,8},{9,10},{11,12},{13,14},{15,16},{17,18},{19,20},..., dimensions={0}, use_global_device_ids=true | all-gather | bytes 1277952 | tf_op jit(solution)/shard_map/all_gather | solution.py:697
  40.1 1.8 %shard_map.69 = (f32[4,18,8,128]{3,2,1,0:T(8,128)S(1)}, f32[12,8,128]{2,1,0:T(8,128)S(1)}, f32[8,8,128]{2,1,0:T(8,128)S(1)}) custom-call(s32[3]{0:T(128)S(1)} %pad_add_fusion.place_ref, f32[18,8,128]{2,1,0:T(8,128)S(1)} %get-tuple-element.21.own_ref, f32[8,8,128]{2,1,0:T(8,128)S(1)} %get-tuple-element.22.packed_ref, f32[2,36,8,128]{3,2,1,0:T(8,128)S(1)} %bitcast.28, ...), custom_call_target="tpu_custom_call" | custom-call | flops 4000000 | bytes 4000000 | tf_op jit(solution)/shard_map/pallas_call | solution.py:670
  41.9 1.9 %all-gather.4 = f32[24,8,128]{2,1,0:T(8,128)S(1)} all-gather(f32[12,8,128]{2,1,0:T(8,128)S(1)} %get-tuple-element.25.send_ref), channel_id=6, replica_groups={{0,1},{2,3},{4,5},{6,7},{8,9},{10,11},{12,13},{14,15},{16,17},{18,19},{..., dimensions={0}, use_global_device_ids=true | all-gather | bytes 147456 | tf_op jit(solution)/shard_map/all_gather | solution.py:697
  43.8 5.3 %all-gather.5 = f32[4,12,8,128]{3,2,1,0:T(8,128)S(1)} all-gather(f32[2,12,8,128]{3,2,1,0:T(8,128)S(1)} %bitcast.39), channel_id=7, replica_groups={{0,64},{128,192},{256,320},{384,448},{512,576},{640,704},{768,832},{896..., dimensions={0}, use_global_device_ids=true | all-gather | bytes 294912 | tf_op jit(solution)/shard_map/all_gather | solution.py:697
  49.0 2.8 %all-gather.6 = f32[4,2,12,8,128]{4,3,2,1,0:T(8,128)S(1)} all-gather(f32[2,2,12,8,128]{4,3,2,1,0:T(8,128)S(1)} %bitcast.46), channel_id=8, replica_groups={{0,1},{2,3},{4,5},{6,7},{8,9},{10,11},{12,13},{14,15},{16,17},{18,19},{..., dimensions={0}, use_global_device_ids=true | all-gather | bytes 589824 | tf_op jit(solution)/shard_map/all_gather | solution.py:697
  51.9 1.4 %shard_map.70 = (f32[18,8,128]{2,1,0:T(8,128)S(1)}, f32[4,18,8,128]{3,2,1,0:T(8,128)S(1)}, f32[8,8,128]{2,1,0:T(8,128)S(1)}) custom-call(s32[3]{0:T(128)S(1)} %pad_add_fusion.place_ref, f32[18,8,128]{2,1,0:T(8,128)S(1)} %get-tuple-element.21.own_ref, f32[4,18,8,128]{3,2,1,0:T(8,128)S(1)} %get-tuple-element.24.halo_ref, ...), custom_call_target="tpu_custom_call" | custom-call | flops 4000000 | bytes 4000000 | tf_op jit(solution)/shard_map/pallas_call | solution.py:670
  53.3 1.9 %all-gather.7 = f32[16,8,128]{2,1,0:T(8,128)S(1)} all-gather(f32[8,8,128]{2,1,0:T(8,128)S(1)} %get-tuple-element.29.packed_ref), channel_id=9, replica_groups={{0,1},{2,3},{4,5},{6,7},{8,9},{10,11},{12,13},{14,15},{16,17},{18,19},{..., dimensions={0}, use_global_device_ids=true | all-gather | bytes 98304 | tf_op jit(solution)/shard_map/all_gather | solution.py:697
  55.1 4.9 %all-gather.8 = f32[4,8,8,128]{3,2,1,0:T(8,128)S(1)} all-gather(f32[2,8,8,128]{3,2,1,0:T(8,128)S(1)} %bitcast.36), channel_id=10, replica_groups={{0,64},{128,192},{256,320},{384,448},{512,576},{640,704},{768,832},{896..., dimensions={0}, use_global_device_ids=true | all-gather | bytes 196608 | tf_op jit(solution)/shard_map/all_gather | solution.py:697
  60.1 2.9 %all-gather.9 = f32[4,2,8,8,128]{4,3,2,1,0:T(8,128)S(1)} all-gather(f32[2,2,8,8,128]{4,3,2,1,0:T(8,128)S(1)} %bitcast.47), channel_id=11, replica_groups={{0,1},{2,3},{4,5},{6,7},{8,9},{10,11},{12,13},{14,15},{16,17},{18,19},{..., dimensions={0}, use_global_device_ids=true | all-gather | bytes 393216 | tf_op jit(solution)/shard_map/all_gather | solution.py:697
  63.6 8.8 %all-gather.10 = f32[42,8,128]{2,1,0:T(8,128)S(1)} all-gather(f32[21,8,128]{2,1,0:T(8,128)S(1)} %shard_map.71), channel_id=12, replica_groups={{1,2},{3,4},{5,6},{7,8},{9,10},{11,12},{13,14},{15,16},{17,18},{19,20},..., dimensions={0}, use_global_device_ids=true | all-gather | bytes 258048 | tf_op jit(solution)/shard_map/all_gather | solution.py:697
  73.2 4.4 %collective-permute-start = (f32[2,18,8,128]{3,2,1,0:T(8,128)S(1)}, f32[2,18,8,128]{3,2,1,0:T(8,128)S(1)}, u32[]{:S(2)}, u32[]{:S(2)}) collective-permute-start(f32[2,18,8,128]{3,2,1,0:T(8,128)S(1)} %get-tuple-element.34.spatial_ref), channel_id=1, source_target_pairs={{0,512},{512,0},{1,513},{513,1},{2,514},{514,2},{3,515},{515,3},{4... | collective-permute-start | bytes 442376 | tf_op jit(solution)/shard_map/ppermute | solution.py:742
  77.7 0.8 shard_map.74
  78.5 1.3 %shard_map.73 = (f32[144,128]{1,0:T(8,128)}, f32[144,128]{1,0:T(8,128)}) custom-call(f32[18,8,128]{2,1,0:T(8,128)S(1)} %get-tuple-element.30.own_ref, f32[4,18,8,128]{3,2,1,0:T(8,128)S(1)} %get-tuple-element.31.halo_ref, f32[8,8,128]{2,1,0:T(8,128)S(1)} %get-tuple-element.29.packed_ref), custom_call_target="tpu_custom_call" | custom-call | flops 4000000 | bytes 4000000 | tf_op jit(solution)/shard_map/pallas_call | solution.py:670
  79.8 1.0 collective-permute-done.spatial_ref.other_ref
  80.8 0.9 shard_map.75
  81.7 1.9 %all-gather.11 = f32[48,8,128]{2,1,0:T(8,128)S(1)} all-gather(f32[24,8,128]{2,1,0:T(8,128)S(1)} %get-tuple-element.37.field_ref.older_ref), channel_id=13, replica_groups={{0,1},{2,3},{4,5},{6,7},{8,9},{10,11},{12,13},{14,15},{16,17},{18,19},{..., dimensions={0}, use_global_device_ids=true | all-gather | bytes 294912 | tf_op jit(solution)/shard_map/all_gather | solution.py:697
  83.6 0.9 shard_map.76.field_ref
  84.5 1.9 %all-gather.12 = f32[48,8,128]{2,1,0:T(8,128)S(1)} all-gather(f32[24,8,128]{2,1,0:T(8,128)S(1)} %shard_map.76.field_ref), channel_id=14, replica_groups={{0,1},{2,3},{4,5},{6,7},{8,9},{10,11},{12,13},{14,15},{16,17},{18,19},{..., dimensions={0}, use_global_device_ids=true | all-gather | bytes 294912 | tf_op jit(solution)/shard_map/all_gather | solution.py:697
  86.4 9.5 %all-gather.13 = f32[48,8,128]{2,1,0:T(8,128)S(1)} all-gather(f32[24,8,128]{2,1,0:T(8,128)S(1)} %shard_map.76.field_ref), channel_id=15, replica_groups={{1,2},{3,4},{5,6},{7,8},{9,10},{11,12},{13,14},{15,16},{17,18},{19,20},..., dimensions={0}, use_global_device_ids=true | all-gather | bytes 294912 | tf_op jit(solution)/shard_map/all_gather | solution.py:697
  96.0 1.9 %shard_map.77 = f32[192,128]{1,0:T(8,128)} custom-call(s32[3]{0:T(128)S(1)} %pad_add_fusion.place_ref, f32[4]{0:T(128)} %coefficients_hbm.1, f32[2,18,8,128]{3,2,1,0:T(8,128)S(1)} %get-tuple-element.34.spatial_ref, f32[2,18,8,128]{3,2,1,0:T(8,128)S(1)} %collective-permute-done.spatial_ref.other_ref, f32[24,8,128]{2,1,0:T(8,128)S(1)} %shard_map.76.field_ref, ...), custom_call_target="tpu_custom_call" | custom-call | flops 4000000 | bytes 4000000 | tf_op jit(solution)/shard_map/pallas_call | solution.py:670
  (5 shorter events, 2.1 us)
Async XLA Ops:
  73.2 7.6 %collective-permute-start = (f32[2,18,8,128]{3,2,1,0:T(8,128)S(1)}, f32[2,18,8,128]{3,2,1,0:T(8,128)S(1)}, u32[]{:S(2)}, u32[]{:S(2)}) collective-permute-start(f32[2,18,8,128]{3,2,1,0:T(8,128)S(1)} %get-tuple-element.34.spatial_ref), channel_id=1, source_target_pairs={{0,512},{512,0},{1,513},{513,1},{2,514},{514,2},{3,515},{515,3},{4... | collective-permute-start | bytes 442376 | tf_op jit(solution)/shard_map/ppermute | solution.py:742

commit v5 on v4

--- a/solution.py
+++ b/solution.py
@@ -277,8 +277,8 @@
 PACKED = (1, 9, 2, 3, 4, 5, 10, 11)
 
 
-def split_kernel(place_ref, links_hbm, momenta_hbm, vectors_hbm, own_ref, packed_ref, send_ref, links_ref, momenta_ref, vectors_ref, sems):
-    half = place_ref[2]
+def split_kernel(place, links_hbm, momenta_hbm, vectors_hbm, own_ref, packed_ref, send_ref, links_ref, momenta_ref, vectors_ref, sems):
+    half = place[2]
     copies = [
         pltpu.make_async_copy(source, target, sems.at[i])
         for i, (source, target) in enumerate(
@@ -311,9 +311,9 @@
             packed_ref[slot, 2 * d : 2 * d + 2, :] = momenta_ref[d * 36 + 2 * c : d * 36 + 2 * c + 2, :]
 
 
-def first_bundle_kernel(place_ref, send_ref, packed_ref, near_ref, sides_ref, out_ref):
+def first_bundle_kernel(place, send_ref, packed_ref, near_ref, sides_ref, out_ref):
     row, _ = iotas()
-    odd_time, odd_space = place_ref[0], place_ref[1]
+    odd_time, odd_space = place[0], place[1]
     first = odd_space == 0
     for c in range(12):
         ahead = sides_ref[odd_time, 1, odd_space, c]
@@ -332,11 +332,11 @@
 
 
 def first_kernel(
-    place_ref, own_ref, packed_ref, near_ref, sides_ref, across_ref,
+    place, own_ref, packed_ref, near_ref, sides_ref, across_ref,
     halo_ref, send_ref, far_packed_ref, forward, work, far_own, far_halo,
 ):
     row, _ = iotas()
-    odd_time, odd_space = place_ref[0], place_ref[1]
+    odd_time, odd_space = place[0], place[1]
     first = odd_space == 0
     x_row = row // 2 == 1
 
@@ -400,11 +400,11 @@
 
 
 def middle_kernel(
-    place_ref, own_ref, halo_ref, send_ref, far_packed_ref, near_ref, sides_ref,
+    place, own_ref, halo_ref, send_ref, far_packed_ref, near_ref, sides_ref,
     new_own_ref, new_halo_ref, next_ref, forward, work,
 ):
     row, _ = iotas()
-    odd_time, odd_space = place_ref[0], place_ref[1]
+    odd_time, odd_space = place[0], place[1]
     first = odd_space == 0
 
     def entry(h, c):
@@ -427,9 +427,9 @@
         next_ref[c] = send_ref[c] - time_step * kick[c]
 
 
-def last_bundle_kernel(place_ref, own_ref, halo_ref, packed_ref, near_ref, sides_ref, out_ref):
+def last_bundle_kernel(place, own_ref, halo_ref, packed_ref, near_ref, sides_ref, out_ref):
     row, _ = iotas()
-    odd_time, odd_space = place_ref[0], place_ref[1]
+    odd_time, odd_space = place[0], place[1]
     first = odd_space == 0
 
     def corner(c):
@@ -449,11 +449,11 @@
 
 
 def last_drift_kernel(
-    place_ref, own_ref, halo_ref, packed_ref, near_ref, sides_ref, across_ref,
+    place, own_ref, halo_ref, packed_ref, near_ref, sides_ref, across_ref,
     new_own_ref, new_halo_ref, spatial_ref,
 ):
     row, _ = iotas()
-    odd_time, odd_space = place_ref[0], place_ref[1]
+    odd_time, odd_space = place[0], place[1]
     first = odd_space == 0
     x_row = row // 2 == 1
 
@@ -549,8 +549,8 @@
                 emit(c * 4 + side * 2 + block, totals[block, c] * (-1.0 / 6.0))
 
 
-def first_hop_kernel(side, place_ref, spatial_ref, field_ref, near_ref, across_ref, *rest):
-    odd_space = place_ref[1]
+def first_hop_kernel(side, place, spatial_ref, field_ref, near_ref, across_ref, *rest):
+    odd_space = place[1]
     first = odd_space == 0
     out_ref, far_out_ref = rest[-2:]
     if side == 1:
@@ -596,8 +596,8 @@
     )
 
 
-def second_hop_kernel(place_ref, spatial_ref, other_ref, field_ref, older_ref, near_ref, far_ref, out_ref):
-    odd_space = place_ref[1]
+def second_hop_kernel(place, spatial_ref, other_ref, field_ref, older_ref, near_ref, far_ref, out_ref):
+    odd_space = place[1]
     first = odd_space == 0
 
     def near(tile):
@@ -617,12 +617,12 @@
 
 
 def last_hop_kernel(
-    place_ref, coefficients_hbm, spatial_ref, other_ref, field_ref, older_ref, oldest_ref, near_ref, across_ref,
+    place, coefficients_hbm, spatial_ref, other_ref, field_ref, older_ref, oldest_ref, near_ref, across_ref,
     out_ref, work, coefficients_ref, sem,
 ):
     copy = pltpu.make_async_copy(coefficients_hbm, coefficients_ref, sem)
     copy.start()
-    odd_space, half = place_ref[1], place_ref[2]
+    odd_space, half = place[1], place[2]
     first = odd_space == 0
 
     def near(tile):
@@ -657,20 +657,26 @@
                     out_ref[pl.ds(block * 96 + c * 4 + h * 2 + side, 4, stride=24), :] = value[4 * side : 4 * side + 4, :]
 
 
-def call(kernel, shapes, inputs, scratch=(), scalars=1, hbm=()):
-    def spec(position):
-        if position < scalars:
-            return pl.BlockSpec(memory_space=pltpu.SMEM)
-        return pl.BlockSpec(memory_space=pltpu.HBM if position in hbm else pltpu.VMEM)
+def here():
+    half = lax.axis_index("grp")
+    t = half * lax.axis_size("ta") + lax.axis_index("ta")
+    return lax.rem(t, 2), lax.rem(lax.axis_index("xyz"), 2), half
+
+
+def call(kernel, shapes, inputs, scratch=(), placed=True, hbm=()):
+    def run(*refs):
+        return kernel(here(), *refs) if placed else kernel(*refs)
 
     inputs = [
         pltpu.with_memory_space_constraint(value, pltpu.HBM) if position in hbm else value
         for position, value in enumerate(inputs)
     ]
     return pl.pallas_call(
-        kernel,
+        run,
         out_shape=[jax.ShapeDtypeStruct(shape, F32) for shape in shapes],
-        in_specs=[spec(position) for position in range(len(inputs))],
+        in_specs=[
+            pl.BlockSpec(memory_space=pltpu.HBM if position in hbm else pltpu.VMEM) for position in range(len(inputs))
+        ],
         out_specs=[pl.BlockSpec(memory_space=pltpu.VMEM)] * len(shapes),
         scratch_shapes=[pltpu.VMEM(shape, F32) if isinstance(shape, tuple) else shape for shape in scratch],
         compiler_params=pltpu.CompilerParams(vmem_limit_bytes=8 << 20),
@@ -696,27 +702,24 @@
     def meet(values, which):
         return lax.all_gather(values, AXES, axis_index_groups=which)
 
-    t = lax.axis_index(("grp", "ta"))
-    x = lax.axis_index("xyz")
-    place = jnp.stack([t % 2, x % 2, lax.axis_index("grp")]).astype(jnp.int32)
     raw = [links.reshape(144, 128), momenta.reshape(144, 128), vectors.reshape(192, 128)]
     own, packed, send = call(
         split_kernel,
         [(18,) + TILE, (8,) + TILE, (36,) + TILE],
-        [place] + raw,
+        raw,
         [value.shape for value in raw] + [pltpu.SemaphoreType.DMA((3,))],
-        hbm=(1, 2, 3),
+        hbm=(0, 1, 2),
     )
     forces = [(3, 18) + TILE, (3, 18) + TILE]
 
     near = meet(send, chip)
     sides = meet(meet(near[:, :12], time), chip)
-    (bundle,) = call(first_bundle_kernel, [(104,) + TILE], [place, send, packed, near, sides])
+    (bundle,) = call(first_bundle_kernel, [(104,) + TILE], [send, packed, near, sides])
     far = meet(bundle, across)
     halo, pushed, far_packed = call(
         first_kernel,
         [(4, 18) + TILE, (12,) + TILE, (8,) + TILE],
-        [place, own, packed, near, sides, far],
+        [own, packed, near, sides, far],
         forces + [(18,) + TILE, (4, 18) + TILE],
     )
     fields, fields_near, fields_far = send, near, far
@@ -726,39 +729,39 @@
     own, halo, packed = call(
         middle_kernel,
         [(18,) + TILE, (4, 18) + TILE, (8,) + TILE],
-        [place, own, halo, pushed, far_packed, near, sides],
+        [own, halo, pushed, far_packed, near, sides],
         forces,
     )
 
     near = meet(packed, chip)
     sides = meet(meet(near, time), chip)
-    (bundle,) = call(last_bundle_kernel, [(21,) + TILE], [place, own, halo, packed, near, sides])
+    (bundle,) = call(last_bundle_kernel, [(21,) + TILE], [own, halo, packed, near, sides])
     own, halo, spatial = call(
         last_drift_kernel,
         [(18,) + TILE, (4, 18) + TILE, (2, 18) + TILE],
-        [place, own, halo, packed, near, sides, meet(bundle, across)],
+        [own, halo, packed, near, sides, meet(bundle, across)],
     )
 
     other = lax.ppermute(spatial, "grp", [(0, 1), (1, 0)])
     vectors_here = [fields, fields_near, fields_far]
     one, far_one = call(
-        functools.partial(first_hop_kernel, 0), [(24,) + TILE] * 2, [place, spatial] + vectors_here
+        functools.partial(first_hop_kernel, 0), [(24,) + TILE] * 2, [spatial] + vectors_here
     )
     new_links, new_momenta = call(
-        last_force_kernel, [(144, 128), (144, 128)], [own, halo, packed], forces, scalars=0
+        last_force_kernel, [(144, 128), (144, 128)], [own, halo, packed], forces, placed=False
     )
     one, far_one = call(
-        functools.partial(first_hop_kernel, 1), [(24,) + TILE] * 2, [place, other] + vectors_here + [one, far_one]
+        functools.partial(first_hop_kernel, 1), [(24,) + TILE] * 2, [other] + vectors_here + [one, far_one]
     )
     (two,) = call(
-        second_hop_kernel, [(24,) + TILE], [place, spatial, other, one, fields, meet(one, chip), far_one]
+        second_hop_kernel, [(24,) + TILE], [spatial, other, one, fields, meet(one, chip), far_one]
     )
     (filtered,) = call(
         last_hop_kernel,
         [(192, 128)],
-        [place, coefficients, spatial, other, two, one, fields, meet(two, chip), meet(two, across)],
+        [coefficients, spatial, other, two, one, fields, meet(two, chip), meet(two, across)],
         [(24,) + TILE, pltpu.SMEM((4,), F32), pltpu.SemaphoreType.DMA],
-        hbm=(1,),
+        hbm=(0,),
     )
     return (
         new_links.reshape(links.shape),

time: 98.2 us -> 93.1 us (0.948)
  Pallas kernels: 12.5 us -> 7.16 us
    pallas_call x11, Pallas kernels: 12.5 us -> 7.16 us  [call(): pl.pallas_call(run, out_shape=[jax.ShapeDtypeStruct(shape, F32) for shape...]
where the time goes in v5:
time: 93.1 us; the launch traced here: 92.8 us
  blocking collectives  79.3 us (85%)
  Pallas kernels  7.16 us (8%)
  starting transfers between devices  4.06 us (4%)
  waiting for transfers between devices  1.53 us (2%)
    all_gather x14, blocking collectives, meet(): return lax.all_gather(values, AXES, axis_index_groups=which)  79.3 us
    pallas_call x11, Pallas kernels, call(): pl.pallas_call(run, out_shape=[jax.ShapeDtypeStruct(shape, F32) for shape...  7.16 us
    ppermute x1, starting transfers between devices, body(): other = lax.ppermute(spatial, 'grp', [(0, 1), (1, 0)])  4.06 us
  transfers between devices with their start and end apart: 1, of which 1 were waited for; matrix products, arithmetic and copies ran while one was open for 0% of the time, Pallas kernels for 2%

profile of v5, /device:TPU:112, one launch (start us, length us, event | category | flops | bytes accessed | tf_op | source)
XLA Modules:
  0.0 92.8 jit_solution(3461574802223449854)
XLA Ops:
  0.6 1.0 %shard_map.67 = (f32[18,8,128]{2,1,0:T(8,128)S(1)}, f32[8,8,128]{2,1,0:T(8,128)S(1)}, f32[36,8,128]{2,1,0:T(8,128)S(1)}) custom-call(f32[144,128]{1,0:T(8,128)} %bitcast.47, f32[144,128]{1,0:T(8,128)} %bitcast.48, f32[192,128]{1,0:T(8,128)} %bitcast.45), custom_call_target="tpu_custom_call" | custom-call | flops 4000000 | bytes 4000000 | tf_op jit(solution)/shard_map/pallas_call | solution.py:674
  1.6 2.0 %all-gather = f32[72,8,128]{2,1,0:T(8,128)S(1)} all-gather(f32[36,8,128]{2,1,0:T(8,128)S(1)} %get-tuple-element.23.refs_0_.refs_1_.refs_3_.refs_5_), channel_id=2, replica_groups={{0,1},{2,3},{4,5},{6,7},{8,9},{10,11},{12,13},{14,15},{16,17},{18,19},{..., dimensions={0}, use_global_device_ids=true | all-gather | bytes 442368 | tf_op jit(solution)/shard_map/all_gather | solution.py:703
  3.7 5.3 %all-gather.1 = f32[4,12,8,128]{3,2,1,0:T(8,128)S(1)} all-gather(f32[2,12,8,128]{3,2,1,0:T(8,128)S(1)} %slice.4), channel_id=3, replica_groups={{0,64},{128,192},{256,320},{384,448},{512,576},{640,704},{768,832},{896..., dimensions={0}, use_global_device_ids=true | all-gather | bytes 294912 | tf_op jit(solution)/shard_map/all_gather | solution.py:703
  9.0 2.8 %all-gather.2 = f32[4,2,12,8,128]{4,3,2,1,0:T(8,128)S(1)} all-gather(f32[2,2,12,8,128]{4,3,2,1,0:T(8,128)S(1)} %bitcast.42), channel_id=4, replica_groups={{0,1},{2,3},{4,5},{6,7},{8,9},{10,11},{12,13},{14,15},{16,17},{18,19},{..., dimensions={0}, use_global_device_ids=true | all-gather | bytes 589824 | tf_op jit(solution)/shard_map/all_gather | solution.py:703
  11.8 27.1 %all-gather.3 = f32[208,8,128]{2,1,0:T(8,128)S(1)} all-gather(f32[104,8,128]{2,1,0:T(8,128)S(1)} %shard_map.68), channel_id=5, replica_groups={{1,2},{3,4},{5,6},{7,8},{9,10},{11,12},{13,14},{15,16},{17,18},{19,20},..., dimensions={0}, use_global_device_ids=true | all-gather | bytes 1277952 | tf_op jit(solution)/shard_map/all_gather | solution.py:703
  38.9 1.2 %shard_map.69 = (f32[4,18,8,128]{3,2,1,0:T(8,128)S(1)}, f32[12,8,128]{2,1,0:T(8,128)S(1)}, f32[8,8,128]{2,1,0:T(8,128)S(1)}) custom-call(f32[18,8,128]{2,1,0:T(8,128)S(1)} %get-tuple-element.21.refs_0_, f32[8,8,128]{2,1,0:T(8,128)S(1)} %get-tuple-element.22.refs_1_, f32[2,36,8,128]{3,2,1,0:T(8,128)S(1)} %bitcast.25, f32[2,2,2,12,8,128]{5,4,3,2,1,0:T(8,128)S(1)} %bitcast.29, ...), custom_call_target="tpu_custom_call" | custom-call | flops 4000000 | bytes 4000000 | tf_op jit(solution)/shard_map/pallas_call | solution.py:674
  40.2 1.9 %all-gather.4 = f32[24,8,128]{2,1,0:T(8,128)S(1)} all-gather(f32[12,8,128]{2,1,0:T(8,128)S(1)} %get-tuple-element.25.refs_2_), channel_id=6, replica_groups={{0,1},{2,3},{4,5},{6,7},{8,9},{10,11},{12,13},{14,15},{16,17},{18,19},{..., dimensions={0}, use_global_device_ids=true | all-gather | bytes 147456 | tf_op jit(solution)/shard_map/all_gather | solution.py:703
  42.1 5.3 %all-gather.5 = f32[4,12,8,128]{3,2,1,0:T(8,128)S(1)} all-gather(f32[2,12,8,128]{3,2,1,0:T(8,128)S(1)} %bitcast.36), channel_id=7, replica_groups={{0,64},{128,192},{256,320},{384,448},{512,576},{640,704},{768,832},{896..., dimensions={0}, use_global_device_ids=true | all-gather | bytes 294912 | tf_op jit(solution)/shard_map/all_gather | solution.py:703
  47.3 2.8 %all-gather.6 = f32[4,2,12,8,128]{4,3,2,1,0:T(8,128)S(1)} all-gather(f32[2,2,12,8,128]{4,3,2,1,0:T(8,128)S(1)} %bitcast.43), channel_id=8, replica_groups={{0,1},{2,3},{4,5},{6,7},{8,9},{10,11},{12,13},{14,15},{16,17},{18,19},{..., dimensions={0}, use_global_device_ids=true | all-gather | bytes 589824 | tf_op jit(solution)/shard_map/all_gather | solution.py:703
  50.1 0.9 shard_map.70
  51.0 1.9 %all-gather.7 = f32[16,8,128]{2,1,0:T(8,128)S(1)} all-gather(f32[8,8,128]{2,1,0:T(8,128)S(1)} %get-tuple-element.29.refs_2_), channel_id=9, replica_groups={{0,1},{2,3},{4,5},{6,7},{8,9},{10,11},{12,13},{14,15},{16,17},{18,19},{..., dimensions={0}, use_global_device_ids=true | all-gather | bytes 98304 | tf_op jit(solution)/shard_map/all_gather | solution.py:703
  52.9 4.9 %all-gather.8 = f32[4,8,8,128]{3,2,1,0:T(8,128)S(1)} all-gather(f32[2,8,8,128]{3,2,1,0:T(8,128)S(1)} %bitcast.33), channel_id=10, replica_groups={{0,64},{128,192},{256,320},{384,448},{512,576},{640,704},{768,832},{896..., dimensions={0}, use_global_device_ids=true | all-gather | bytes 196608 | tf_op jit(solution)/shard_map/all_gather | solution.py:703
  57.8 2.9 %all-gather.9 = f32[4,2,8,8,128]{4,3,2,1,0:T(8,128)S(1)} all-gather(f32[2,2,8,8,128]{4,3,2,1,0:T(8,128)S(1)} %bitcast.44), channel_id=11, replica_groups={{0,1},{2,3},{4,5},{6,7},{8,9},{10,11},{12,13},{14,15},{16,17},{18,19},{..., dimensions={0}, use_global_device_ids=true | all-gather | bytes 393216 | tf_op jit(solution)/shard_map/all_gather | solution.py:703
  60.8 9.0 %all-gather.10 = f32[42,8,128]{2,1,0:T(8,128)S(1)} all-gather(f32[21,8,128]{2,1,0:T(8,128)S(1)} %shard_map.71), channel_id=12, replica_groups={{1,2},{3,4},{5,6},{7,8},{9,10},{11,12},{13,14},{15,16},{17,18},{19,20},..., dimensions={0}, use_global_device_ids=true | all-gather | bytes 258048 | tf_op jit(solution)/shard_map/all_gather | solution.py:703
  70.1 4.1 %collective-permute-start = (f32[2,18,8,128]{3,2,1,0:T(8,128)S(1)}, f32[2,18,8,128]{3,2,1,0:T(8,128)S(1)}, u32[]{:S(2)}, u32[]{:S(2)}) collective-permute-start(f32[2,18,8,128]{3,2,1,0:T(8,128)S(1)} %get-tuple-element.34.refs_0_.refs_1_), channel_id=1, source_target_pairs={{0,512},{512,0},{1,513},{513,1},{2,514},{514,2},{3,515},{515,3},{4... | collective-permute-start | bytes 442376 | tf_op jit(solution)/shard_map/ppermute | solution.py:745
  74.2 0.3 shard_map.74
  74.5 1.3 %shard_map.73 = (f32[144,128]{1,0:T(8,128)}, f32[144,128]{1,0:T(8,128)}) custom-call(f32[18,8,128]{2,1,0:T(8,128)S(1)} %get-tuple-element.30.refs_0_, f32[4,18,8,128]{3,2,1,0:T(8,128)S(1)} %get-tuple-element.31.refs_1_, f32[8,8,128]{2,1,0:T(8,128)S(1)} %get-tuple-element.29.refs_2_), custom_call_target="tpu_custom_call" | custom-call | flops 4000000 | bytes 4000000 | tf_op jit(solution)/shard_map/pallas_call | solution.py:674
  75.8 1.5 %collective-permute-done.refs_0_.refs_1_.refs_2_ = f32[2,18,8,128]{3,2,1,0:T(8,128)S(1)} collective-permute-done((f32[2,18,8,128]{3,2,1,0:T(8,128)S(1)}, f32[2,18,8,128]{3,2,1,0:T(8,128)S(1)}, u32[]{:S(2)}, u32[]{:S(2)}) %collective-permute-start) | collective-permute-done | bytes 147488 | tf_op jit(solution)/shard_map/ppermute | solution.py:745
  77.3 0.3 shard_map.75
  77.6 1.9 %all-gather.11 = f32[48,8,128]{2,1,0:T(8,128)S(1)} all-gather(f32[24,8,128]{2,1,0:T(8,128)S(1)} %get-tuple-element.37.refs_2_.refs_4_), channel_id=13, replica_groups={{0,1},{2,3},{4,5},{6,7},{8,9},{10,11},{12,13},{14,15},{16,17},{18,19},{..., dimensions={0}, use_global_device_ids=true | all-gather | bytes 294912 | tf_op jit(solution)/shard_map/all_gather | solution.py:703
  79.6 0.3 shard_map.76.refs_3_
  79.9 1.9 %all-gather.12 = f32[48,8,128]{2,1,0:T(8,128)S(1)} all-gather(f32[24,8,128]{2,1,0:T(8,128)S(1)} %shard_map.76.refs_3_), channel_id=14, replica_groups={{0,1},{2,3},{4,5},{6,7},{8,9},{10,11},{12,13},{14,15},{16,17},{18,19},{..., dimensions={0}, use_global_device_ids=true | all-gather | bytes 294912 | tf_op jit(solution)/shard_map/all_gather | solution.py:703
  81.8 9.5 %all-gather.13 = f32[48,8,128]{2,1,0:T(8,128)S(1)} all-gather(f32[24,8,128]{2,1,0:T(8,128)S(1)} %shard_map.76.refs_3_), channel_id=15, replica_groups={{1,2},{3,4},{5,6},{7,8},{9,10},{11,12},{13,14},{15,16},{17,18},{19,20},..., dimensions={0}, use_global_device_ids=true | all-gather | bytes 294912 | tf_op jit(solution)/shard_map/all_gather | solution.py:703
  91.3 1.5 %shard_map.77 = f32[192,128]{1,0:T(8,128)} custom-call(f32[4]{0:T(128)} %refs_0_.1, f32[2,18,8,128]{3,2,1,0:T(8,128)S(1)} %get-tuple-element.34.refs_0_.refs_1_, f32[2,18,8,128]{3,2,1,0:T(8,128)S(1)} %collective-permute-done.refs_0_.refs_1_.refs_2_, f32[24,8,128]{2,1,0:T(8,128)S(1)} %shard_map.76.refs_3_, ...), custom_call_target="tpu_custom_call" | custom-call | flops 4000000 | bytes 4000000 | tf_op jit(solution)/shard_map/pallas_call | solution.py:674
  (4 shorter events, 0.4 us)
Async XLA Ops:
  70.1 7.2 %collective-permute-start = (f32[2,18,8,128]{3,2,1,0:T(8,128)S(1)}, f32[2,18,8,128]{3,2,1,0:T(8,128)S(1)}, u32[]{:S(2)}, u32[]{:S(2)}) collective-permute-start(f32[2,18,8,128]{3,2,1,0:T(8,128)S(1)} %get-tuple-element.34.refs_0_.refs_1_), channel_id=1, source_target_pairs={{0,512},{512,0},{1,513},{513,1},{2,514},{514,2},{3,515},{515,3},{4... | collective-permute-start | bytes 442376 | tf_op jit(solution)/shard_map/ppermute | solution.py:745
